TPU v7x, 128 devices: a whole 4x4x4 slice. The times are simulated.
128 devices in a mesh: queue: 32 (over y, x, z_lo), head: 4 (over z_hi, core).
Axes of the slice: x: 4, y: 4, z: 4 (z_hi: 2, z_lo: 2; z = z_hi * 2 + z_lo), core: 2. Of those that a mesh axis runs over, the one named last changes fastest.
Arguments:
- latents: bfloat16 [64, 384, 5120], P('queue'), may hold values from -6 to 6
- control: bfloat16 [64, 384, 5120], P('queue'), may hold values from -3 to 3
- levels: int32 [64], P('queue'), may hold values from 0 to 63
- window_mask: int32 [64, 2], P('queue'), may hold values 0 or 1
- modulation: float32 [64, 3, 5120], replicated, may hold values from -3 to 3
- w_query: bfloat16 [5120, 2560], P('queue', 'head'), may hold values from -1 to 1
- w_key: bfloat16 [5120, 2560], P('queue', 'head'), may hold values from -1 to 1
- w_value: bfloat16 [5120, 2560], P('queue', 'head'), may hold values from -0.078125 to 0.078125
- w_out: bfloat16 [2560, 5120], P('head', 'queue'), may hold values from -0.125 to 0.125
- q_gain: float32 [2560], P('head'), may hold values from 0.6 to 8
- k_gain: float32 [2560], P('head'), may hold values from 0.6 to 8
Outputs:
- next_queue: float32 [64, 384, 5120], P('queue', None, 'head')
All inputs are finite; a program needn't handle non-finite values. No bound on the sum of `window_mask` on one device may be relied on, other than what follows from the above.
Results may differ from a plain program's by a relative error of at most 0.019.
The roundings to bfloat16 on the way count: a program that leaves them out, or rounds other values in their place, can miss the bound.
Values may be sent and summed in bfloat16 or wider, within the bound.
A program may use at most 192 MiB of HBM per device.

v0:
```python
import jax
import jax.numpy as jnp
from jax import lax
from jax.sharding import PartitionSpec as P

HD = 128


def from_behind(value, axis, by):
    peers = lax.axis_size(axis)
    pairs = [(i, i + by) for i in range(peers) if 0 <= i + by < peers]
    return lax.ppermute(value, axis, pairs)


def shifted(value, axis, steps):
    count = lax.axis_size(axis)
    pairs = [(source, (source + steps) % count) for source in range(count)]
    return lax.ppermute(value, axis, pairs)


def layer_norm(hidden):
    center = hidden - jnp.mean(hidden, axis=-1, keepdims=True)
    variance = jnp.mean(center * center, axis=-1, keepdims=True)
    return center * lax.rsqrt(variance + 1e-06)


def apply_gain(values, square_sum, total_width, gain):
    floats = values.astype(jnp.float32)
    return (floats * lax.rsqrt(square_sum[:, None] / total_width + 1e-06) * gain).astype(
        jnp.bfloat16
    )


def row_squares(values):
    floats = values.astype(jnp.float32)
    return jnp.sum(floats * floats, axis=-1)


def shards(
    latents,
    control,
    levels,
    window_mask,
    modulation,
    w_query,
    w_key,
    w_value,
    w_out,
    q_gain,
    k_gain,
):
    nchunk, row_count, model_width = latents.shape
    level_count = modulation.shape[0]
    local_cols = w_query.shape[1]
    heads_local = local_cols // HD
    head_count = lax.axis_size("head")
    total_width = local_cols * head_count
    owner_index = lax.axis_index("queue")
    head_index = lax.axis_index("head")
    first_span = owner_index * nchunk
    hidden = latents.astype(jnp.float32) + control.astype(jnp.float32)
    onehot = (levels[:, None] == jnp.arange(level_count, dtype=jnp.int32)[None, :]).astype(
        jnp.float32
    )
    level_mods = jnp.dot(
        onehot, modulation.reshape(level_count, 3 * model_width), precision=lax.Precision.HIGHEST
    ).reshape(nchunk, 3, model_width)
    normed = (
        layer_norm(hidden) * (1.0 + level_mods[:, 1][:, None, :]) + level_mods[:, 0][:, None, :]
    ).astype(jnp.bfloat16)
    flat_rows = normed.reshape(nchunk * row_count, model_width)
    row_total = nchunk * row_count
    pieces = (
        lax.all_gather(w_query, "queue", axis=0, tiled=True),
        lax.all_gather(w_key, "queue", axis=0, tiled=True),
        lax.all_gather(w_value, "queue", axis=0, tiled=True),
    )
    query, keyproj, valueproj = tuple(
        (
            jnp.dot(flat_rows, piece_rows, preferred_element_type=jnp.float32)
            for piece_rows in pieces
        )
    )
    query = query.astype(jnp.bfloat16)
    keyproj = keyproj.astype(jnp.bfloat16)
    valueproj = valueproj.astype(jnp.bfloat16)
    query_sq, key_sq = lax.psum((row_squares(query), row_squares(keyproj)), "head")
    qhat = apply_gain(query, query_sq, total_width, q_gain)
    own_keys = apply_gain(keyproj, key_sq, total_width, k_gain)
    prior_keys, prior_values = from_behind((own_keys, valueproj), "queue", 1)
    key_stack = jnp.concatenate([prior_keys, own_keys], axis=0).reshape(
        2 * nchunk, row_count, heads_local, HD
    )
    value_stack = jnp.concatenate([prior_values, valueproj], axis=0).reshape(
        2 * nchunk, row_count, heads_local, HD
    )
    key_windows = jnp.stack(
        [
            key_stack[nchunk + index_span - 2 : nchunk + index_span + 1]
            for index_span in range(nchunk)
        ]
    ).reshape(nchunk, 3 * row_count, heads_local, HD)
    value_windows = jnp.stack(
        [
            value_stack[nchunk + index_span - 2 : nchunk + index_span + 1]
            for index_span in range(nchunk)
        ]
    ).reshape(nchunk, 3 * row_count, heads_local, HD)
    span_ids = first_span + jnp.arange(nchunk, dtype=jnp.int32)
    seen_far = (window_mask[:, 0] == 1) & (span_ids >= 2)
    seen_near = (window_mask[:, 1] == 1) & (span_ids >= 1)
    seen = jnp.stack([seen_far, seen_near, jnp.ones((nchunk,), dtype=bool)], axis=1)
    key_seen = jnp.repeat(seen, row_count, axis=1)
    query_spans = qhat.reshape(nchunk, row_count, heads_local, HD)
    scores = jnp.einsum(
        "cqhd,ckhd->chqk", query_spans, key_windows, preferred_element_type=jnp.float32
    ) * HD ** (-0.5)
    scores = jnp.where(key_seen[:, None, None, :], scores, -1e30)
    top = jnp.max(scores, axis=-1, keepdims=True)
    expo = jnp.exp(scores - top)
    prob_bf = (expo / jnp.sum(expo, axis=-1, keepdims=True)).astype(jnp.bfloat16)
    attended = jnp.einsum(
        "chqk,ckhd->cqhd", prob_bf, value_windows, preferred_element_type=jnp.float32
    )
    attended = attended.astype(jnp.bfloat16).reshape(row_total, local_cols)
    partial_out = jnp.dot(
        attended,
        lax.all_gather(w_out, "queue", axis=1, tiled=True),
        preferred_element_type=jnp.float32,
    )
    col_width = model_width // head_count
    hidden_cols = lax.dynamic_slice_in_dim(hidden, head_index * col_width, col_width, 2)
    gate_cols = lax.dynamic_slice_in_dim(level_mods[:, 2], head_index * col_width, col_width, 1)
    branch = (
        lax.psum_scatter(partial_out.astype(jnp.bfloat16), "head", scatter_dimension=1, tiled=True)
        .astype(jnp.float32)
        .reshape(nchunk, row_count, col_width)
    )
    updated = hidden_cols + gate_cols[:, None, :] * branch
    arrived = shifted(updated[nchunk - 1].astype(jnp.bfloat16), "queue", 1).astype(jnp.float32)
    return jnp.concatenate([arrived[None], updated[: nchunk - 1]], axis=0)


def solution(mesh):
    placed = (
        P("queue", None, None),
        P("queue", None, None),
        P("queue"),
        P("queue", None),
        P(),
        P("queue", "head"),
        P("queue", "head"),
        P("queue", "head"),
        P("head", "queue"),
        P("head"),
        P("head"),
    )
    return jax.shard_map(
        shards, mesh=mesh, in_specs=placed, out_specs=P("queue", None, "head"), check_vma=False
    )
```

profile of v0, /device:TPU:0, one launch (start us, length us, event | category | flops | bytes accessed | tf_op | source)
XLA Modules:
  0.0 834.2 jit_solution(3768649909468280332)
XLA Ops:
  9.4 13.7 %convert_add_fusion = (f32[2,384,5120]{2,1,0:T(8,128)}, f32[2,384]{1,0:T(2,128)S(1)}) fusion(bf16[2,384,5120]{2,1,0:T(8,128)(2,1)} %param.12, bf16[2,384,5120]{2,1,0:T(8,128)(2,1)} %param.11), kind=kLoop, calls=%fused_computation.6 | loop fusion | flops 15727872 | bytes 31460352 | tf_op jit(solution)/shard_map/add | solution.py:61
  23.1 6.4 multiply_reduce_fusion
  29.8 3.5 fusion.6
  33.3 10.8 %add_convert_fusion = bf16[2,384,5120]{2,1,0:T(8,128)(2,1)} fusion(f32[2,5120]{1,0:T(2,128)S(1)} %get-tuple-element.14, f32[2,5120]{1,0:T(2,128)S(1)} %get-tuple-element.15, f32[2,384]{1,0:T(2,128)S(1)} %add_rsqrt_fusion.2, f32[2,384]{1,0:T(2,128)S(1)} %broadcast_multiply_fusion, bf16[2,384,5120]{2,1,0:T(8,128)(2,1)} %param.12, bf16[2,384,5120]{2,1,0:T(8,128)(2,1)} %param.11), kind=kLoop, calls=%fused_computation.4 | loop fusion | flops 31457280 | bytes 23681024 | tf_op jit(solution)/shard_map/convert_element_type | solution.py:70
  44.1 132.3 %all-gather.7.cloned.1.call-done = bf16[5120,640]{1,0:T(8,128)(2,1)} async-done(((bf16[160,640]{1,0:T(8,128)(2,1)}), bf16[5120,640]{1,0:T(8,128)(2,1)}) %all-gather.7.cloned.1.call-update) | async-done | bytes 6553616 | tf_op jit(solution)/shard_map/all_gather | solution.py:74
  176.4 10.4 %fusion.17 = (f32[768]{0:T(1024)S(1)}, bf16[768,640]{0,1:T(8,128)(2,1)S(1)}) fusion(bf16[768,5120]{1,0:T(8,128)(2,1)} %bitcast.59, bf16[5120,640]{1,0:T(8,128)(2,1)} %all-gather.7.cloned.1.call-done), kind=kOutput, calls=%fused_computation.30 | convolution fusion | flops 5035129856 | bytes 15404032 | tf_op jit(solution)/shard_map/dot_general | solution.py:80
  186.8 153.5 %all-gather.9.cloned.1.call-done = bf16[5120,640]{1,0:T(8,128)(2,1)} async-done(((bf16[160,640]{1,0:T(8,128)(2,1)}), bf16[5120,640]{1,0:T(8,128)(2,1)}) %all-gather.9.cloned.1.call-update) | async-done | bytes 6553616 | tf_op jit(solution)/shard_map/all_gather | solution.py:75
  340.4 10.6 %fusion.20 = (f32[768]{0:T(1024)S(1)}, bf16[768,640]{1,0:T(8,128)(2,1)S(1)}) fusion(bf16[768,5120]{1,0:T(8,128)(2,1)} %bitcast.60, bf16[5120,640]{1,0:T(8,128)(2,1)} %all-gather.9.cloned.1.call-done), kind=kOutput, calls=%fused_computation.33 | convolution fusion | flops 5035129856 | bytes 15404032 | tf_op jit(solution)/shard_map/dot_general | solution.py:80
  351.0 7.7 all-reduce
  359.1 2.4 collective-permute-start.1
  361.4 163.7 %all-gather.5.cloned.1.call-done = bf16[5120,640]{1,0:T(8,128)(2,1)} async-done(((bf16[160,640]{1,0:T(8,128)(2,1)}), bf16[5120,640]{1,0:T(8,128)(2,1)}) %all-gather.5.cloned.1.call-update) | async-done | bytes 6553616 | tf_op jit(solution)/shard_map/all_gather | solution.py:76
  525.1 11.3 %convolution_convert_fusion.3 = bf16[768,640]{1,0:T(8,128)(2,1)} fusion(bf16[768,5120]{1,0:T(8,128)(2,1)} %bitcast.61, bf16[5120,640]{1,0:T(8,128)(2,1)} %all-gather.5.cloned.1.call-done), kind=kOutput, calls=%fused_computation.48 | convolution fusion | flops 5033656320 | bytes 15400960 | tf_op jit(solution)/shard_map/dot_general | solution.py:80
  536.4 2.5 collective-permute-start
  544.6 3.6 copy.23
  551.2 12.5 %collective-permute-done = bf16[768,640]{1,0:T(8,128)(2,1)} collective-permute-done((bf16[768,640]{1,0:T(8,128)(2,1)}, bf16[768,640]{1,0:T(8,128)(2,1)}, u32[]{:S(2)}, u32[]{:S(2)}) %collective-permute-start) | collective-permute-done | bytes 983072 | tf_op jit(solution)/shard_map/ppermute | solution.py:12
  565.8 2.2 copy.19
  569.0 14.5 %fusion.56 = (f32[2,5,384]{2,1,0:T(8,128)S(1)}, f32[2,5,384,1152]{3,2,1,0:T(8,128)}) fusion(pred[2,1152]{1,0:T(4,128)(4,1)S(1)} %bitcast.69, bf16[1,1152,5,128]{3,1,2,0:T(8,128)(2,1)} %copy.24, bf16[1,1152,5,128]{3,1,2,0:T(8,128)(2,1)} %copy.23, bf16[2,384,5,128]{1,0,3,2:T(2,128)(2,1)} %reshape.85), kind=kOutput, calls=%fused_computation.78 | convolution fusion | flops 1151632512 | bytes 21644544 | tf_op jit(solution)/shard_map/sub | solution.py:120
  583.5 7.8 fusion.32
  592.5 114.0 %all-gather.11.cloned.1.call-done = bf16[640,5120]{0,1:T(8,128)(2,1)} async-done(((bf16[640,160]{0,1:T(8,128)(2,1)}), bf16[640,5120]{0,1:T(8,128)(2,1)}) %all-gather.11.cloned.1.call-update) | async-done | bytes 6553616 | tf_op jit(solution)/shard_map/all_gather | solution.py:128
  706.4 11.4 %convolution_convert_fusion = bf16[768,5120]{1,0:T(8,128)(2,1)} fusion(bf16[768,640]{0,1:T(8,128)(2,1)S(1)} %bitcast.68, bf16[640,5120]{0,1:T(8,128)(2,1)} %all-gather.11.cloned.1.call-done), kind=kOutput, calls=%fused_computation.12 | convolution fusion | flops 5037096960 | bytes 15400960 | tf_op jit(solution)/shard_map/dot_general | solution.py:126
  717.9 76.6 %reduce-scatter.2.cloned.1.call-done = bf16[768,1280]{1,0:T(8,128)(2,1)} async-done(((bf16[768,5120]{1,0:T(8,128)(2,1)}), bf16[768,1280]{1,0:T(8,128)(2,1)}) %reduce-scatter.2.cloned.1.call-update) | async-done | bytes 1966096 | tf_op jit(solution)/shard_map/reduce_scatter | solution.py:135
  794.6 3.1 fusion.9
  798.6 26.8 %collective-permute-done.2 = bf16[384,1280]{1,0:T(8,128)(2,1)S(1)} collective-permute-done((bf16[384,1280]{1,0:T(8,128)(2,1)S(1)}, bf16[384,1280]{1,0:T(8,128)(2,1)S(1)}, u32[]{:S(2)}, u32[]{:S(2)}) %collective-permute-start.2) | collective-permute-done | bytes 983072 | tf_op jit(solution)/shard_map/ppermute | solution.py:18
  825.5 2.2 pad_maximum_fusion
  (54 shorter events, 17.4 us)
Async XLA Ops:
  6.5 169.8 %all-gather.7.cloned.1.call-start = ((), (), s32[]{:S(2)}) async-start(), calls=%async_computation.2 | async-start | bytes 6758400 | tf_op jit(solution)/shard_map/all_gather | solution.py:74
  7.3 333.1 %all-gather.9.cloned.1.call-start = ((), (), s32[]{:S(2)}) async-start(), calls=%async_computation.3 | async-start | bytes 6758400 | tf_op jit(solution)/shard_map/all_gather | solution.py:75
  8.0 517.1 %all-gather.5.cloned.1.call-start = ((), (), s32[]{:S(2)}) async-start(), calls=%async_computation.1 | async-start | bytes 6758400 | tf_op jit(solution)/shard_map/all_gather | solution.py:76
  8.7 697.7 %all-gather.11.cloned.1.call-start = ((), (), s32[]{:S(2)}) async-start(), calls=%async_computation.4 | async-start | bytes 6758400 | tf_op jit(solution)/shard_map/all_gather | solution.py:128
  9.3 785.2 %reduce-scatter.2.cloned.1.call-start = ((), (), s32[]{:S(2)}) async-start(), calls=%async_computation.5 | async-start | bytes 9830400 | tf_op jit(solution)/shard_map/reduce_scatter | solution.py:135
  9.4 13.7 %slice-start = ((s8[7864320]{0:T(1024)(128)(4,1)}), s8[4194304]{0:T(1024)(128)(4,1)S(1)}, s32[]{:S(2)}) async-start(s8[7864320]{0:T(1024)(128)(4,1)} %bitcast.57), calls=%async_computation.6 | async-start | bytes 8388608
  9.4 13.7 %slice-start.1 = ((s8[7864320]{0:T(1024)(128)(4,1)}), s8[3670016]{0:T(1024)(128)(4,1)S(1)}, s32[]{:S(2)}) async-start(s8[7864320]{0:T(1024)(128)(4,1)} %bitcast.57), calls=%async_computation.7 | async-start | bytes 7340032
  23.1 6.4 copy-start.4
  23.1 6.7 copy-start.5
  186.8 171.9 %copy-start.2 = (f32[640]{0:T(1024)S(1)}, f32[640]{0:T(1024)}, u32[]{:S(2)}) copy-start(f32[640]{0:T(1024)} %param.21) | copy-start | bytes 7684
  359.0 177.3 %copy-start = (bf16[768,640]{1,0:T(8,128)(2,1)}, bf16[768,640]{1,0:T(8,128)(2,1)S(1)}, u32[]{:S(2)}) copy-start(bf16[768,640]{1,0:T(8,128)(2,1)S(1)} %fusion.22) | copy-start | bytes 2949124
  359.0 179.9 %copy-start.3 = (f32[640]{0:T(1024)S(1)}, f32[640]{0:T(1024)}, u32[]{:S(2)}) copy-start(f32[640]{0:T(1024)} %param.20) | copy-start | bytes 7684
  359.1 181.4 %collective-permute-start.1 = (bf16[768,640]{1,0:T(8,128)(2,1)S(1)}, bf16[768,640]{1,0:T(8,128)(2,1)}, u32[]{:S(2)}, u32[]{:S(2)}) collective-permute-start(bf16[768,640]{1,0:T(8,128)(2,1)S(1)} %fusion.22), channel_id=1, source_target_pairs={{0,4},{4,8},{8,12},{12,16},{16,20},{20,24},{24,28},{28,32},{32,36}... | collective-permute-start | bytes 2949128 | tf_op jit(solution)/shard_map/ppermute | solution.py:12
  536.4 27.4 %collective-permute-start = (bf16[768,640]{1,0:T(8,128)(2,1)}, bf16[768,640]{1,0:T(8,128)(2,1)}, u32[]{:S(2)}, u32[]{:S(2)}) collective-permute-start(bf16[768,640]{1,0:T(8,128)(2,1)} %convolution_convert_fusion.3), channel_id=1, source_target_pairs={{0,4},{4,8},{8,12},{12,16},{16,20},{20,24},{24,28},{28,32},{32,36}... | collective-permute-start | bytes 2949128 | tf_op jit(solution)/shard_map/ppermute | solution.py:12
  569.0 14.5 %copy-start.1 = (bf16[1152,640]{0,1:T(8,128)(2,1)S(1)}, bf16[1152,640]{0,1:T(8,128)(2,1)}, u32[]{:S(2)}) copy-start(bf16[1152,640]{0,1:T(8,128)(2,1)} %copy.19) | copy-start | bytes 4423684
  797.8 27.6 %collective-permute-start.2 = (bf16[384,1280]{1,0:T(8,128)(2,1)S(1)}, bf16[384,1280]{1,0:T(8,128)(2,1)S(1)}, u32[]{:S(2)}, u32[]{:S(2)}) collective-permute-start(bf16[384,1280]{1,0:T(8,128)(2,1)S(1)} %fusion.35), channel_id=1, source_target_pairs={{0,4},{4,8},{8,12},{12,16},{16,20},{20,24},{24,28},{28,32},{32,36}... | collective-permute-start | bytes 2949128 | tf_op jit(solution)/shard_map/ppermute | solution.py:18
Sparse Core Ops, SparseCore 0:
  9.0 167.3 all-gather.6
  178.0 162.3 all-gather.8
  342.0 183.0 all-gather.4
  526.6 179.8 all-gather.10
  718.0 76.5 reduce-scatter.1
where the time goes:
time: 835 us; the launch traced here: 834 us
  waiting for transfers between devices  682 us (82%)
  matrix products  69.5 us (8%)
  other arithmetic  41.2 us (5%)
  local copies, waits for them, and re-layouts  14.7 us (2%)
  between operations  13.4 us (2%)
    all_gather x1, waiting for transfers between devices, shards(): lax.all_gather(w_value, 'queue', axis=0, tiled=True)  164 us
    all_gather x1, waiting for transfers between devices, shards(): lax.all_gather(w_key, 'queue', axis=0, tiled=True)  154 us
    all_gather x1, waiting for transfers between devices, shards(): lax.all_gather(w_query, 'queue', axis=0, tiled=True)  132 us
    all_gather x1, waiting for transfers between devices, shards(): lax.all_gather(w_out, 'queue', axis=1, tiled=True)  114 us
    reduce_scatter x1, waiting for transfers between devices, shards(): lax.psum_scatter(partial_out.astype(jnp.bfloat16), 'head', scatter_dimens...  76.6 us
    dot_general x3, matrix products, shards(): jnp.dot(flat_rows, piece_rows, preferred_element_type=jnp.float32)  32.4 us
    ppermute x1, waiting for transfers between devices, shifted(): return lax.ppermute(value, axis, pairs)  26.8 us
  transfers between devices with their start and end apart: 8, of which 7 were waited for; matrix products, arithmetic and copies ran while one was open for 13% of the time, Pallas kernels for 0%

commit v1 on v0

--- a/solution.py
+++ b/solution.py
@@ -1,9 +1,151 @@
+import functools
+
 import jax
 import jax.numpy as jnp
 from jax import lax
+from jax.experimental import pallas as pl
+from jax.experimental.pallas import tpu as pltpu
 from jax.sharding import PartitionSpec as P
 
 HD = 128
+MESH = pl.DeviceIdType.MESH
+
+
+def queue_at(x, y, zl):
+    return ((y % 4) * 4 + x % 4) * 2 + zl
+
+
+def gather_kernel(wq, wk, wv, wo, oq, ok, ov, oo, lsem, zs, zr, asnd, arcv, bsnd, brcv):
+    q = lax.axis_index("queue")
+    h = lax.axis_index("head")
+    zl = q % 2
+    x = (q // 2) % 4
+    y = q // 8
+    srcs = (wq, wk, wv, wo)
+    dsts = (oq, ok, ov, oo)
+
+    def near(axis, by):
+        return (x + by, y) if axis == 0 else (x, y + by)
+
+    barrier = pltpu.get_barrier_semaphore()
+    peers = [(queue_at(x, y, 1 - zl), h)]
+    for axis in (0, 1):
+        for by in (1, 2, 3):
+            px, py = near(axis, by)
+            peers.append((queue_at(px, py, zl), h))
+    for peer in peers:
+        pl.semaphore_signal(barrier, inc=1, device_id=peer, device_id_type=MESH)
+    pl.semaphore_wait(barrier, len(peers))
+
+    def rows(ref, first, count):
+        return ref.at[pl.ds(first * 160, count * 160), :]
+
+    sends = []
+    locals_ = []
+    for m in range(4):
+        c = pltpu.make_async_copy(srcs[m], rows(dsts[m], q, 1), lsem.at[m])
+        c.start()
+        locals_.append(c)
+
+    def remote(src, dst, ss, rs, dev):
+        return pltpu.make_async_remote_copy(
+            src_ref=src, dst_ref=dst, send_sem=ss, recv_sem=rs, device_id=dev, device_id_type=MESH
+        )
+
+    zcopies = []
+    for m in range(4):
+        c = remote(srcs[m], rows(dsts[m], q, 1), zs.at[m], zr.at[m], (queue_at(x, y, 1 - zl), h))
+        c.start()
+        zcopies.append(c)
+        sends.append(c)
+    first_axis = (0, 0, 1, 1)
+
+    def step_a(m, which, sender):
+        axis = first_axis[m]
+        for by in (1, 3, 2):
+            px, py = near(axis, by)
+            qs = queue_at(x, y, zl if which == 0 else 1 - zl)
+            src = srcs[m] if which == 0 else rows(dsts[m], qs, 1)
+            c = remote(
+                src,
+                rows(dsts[m], qs, 1),
+                asnd.at[m, which, by - 1],
+                arcv.at[m, which, by - 1],
+                (queue_at(px, py, zl), h),
+            )
+            c.start()
+            sends.append(c)
+
+    def step_b(m, frm):
+        axis = first_axis[m]
+        sx, sy = near(axis, -frm)
+        block = rows(dsts[m], queue_at(sx, sy, 0), 2)
+        for by in (1, 3, 2):
+            px, py = near(1 - axis, by)
+            c = remote(
+                block,
+                block,
+                bsnd.at[m, frm, by - 1],
+                brcv.at[m, frm, by - 1],
+                (queue_at(px, py, zl), h),
+            )
+            c.start()
+            sends.append(c)
+
+    for m in range(4):
+        step_a(m, 0, sends)
+    for m in range(4):
+        zcopies[m].wait_recv()
+        step_a(m, 1, sends)
+    for m in range(4):
+        locals_[m].wait()
+        step_b(m, 0)
+    for by in (1, 3, 2):
+        for m in range(4):
+            sx, sy = near(first_axis[m], -by)
+            for which in (0, 1):
+                qs = queue_at(sx, sy, zl if which == 0 else 1 - zl)
+                block = rows(dsts[m], qs, 1)
+                remote(
+                    block, block, asnd.at[m, which, by - 1], arcv.at[m, which, by - 1], (q, h)
+                ).wait_recv()
+            step_b(m, by)
+    for frm in range(4):
+        for by in (1, 3, 2):
+            for m in range(4):
+                axis = first_axis[m]
+                sx, sy = near(axis, -frm)
+                if axis == 0:
+                    sy = sy - by
+                else:
+                    sx = sx - by
+                block = rows(dsts[m], queue_at(sx, sy, 0), 2)
+                remote(
+                    block, block, bsnd.at[m, frm, by - 1], brcv.at[m, frm, by - 1], (q, h)
+                ).wait_recv()
+    for c in sends:
+        c.wait_send()
+
+
+def gather_weights(wq, wk, wv, wo_t):
+    out = jax.ShapeDtypeStruct((5120, 640), jnp.bfloat16)
+    return pl.pallas_call(
+        gather_kernel,
+        out_shape=[out] * 4,
+        in_specs=[pl.BlockSpec(memory_space=pl.ANY)] * 4,
+        out_specs=[pl.BlockSpec(memory_space=pl.ANY)] * 4,
+        scratch_shapes=[
+            pltpu.SemaphoreType.DMA((4,)),
+            pltpu.SemaphoreType.DMA((4,)),
+            pltpu.SemaphoreType.DMA((4,)),
+            pltpu.SemaphoreType.DMA((4, 2, 3)),
+            pltpu.SemaphoreType.DMA((4, 2, 3)),
+            pltpu.SemaphoreType.DMA((4, 4, 3)),
+            pltpu.SemaphoreType.DMA((4, 4, 3)),
+        ],
+        compiler_params=pltpu.CompilerParams(collective_id=0, has_side_effects=True),
+        name="gather_weights",
+    )(wq, wk, wv, wo_t)
 
 
 def from_behind(value, axis, by):
@@ -70,11 +212,8 @@
     ).astype(jnp.bfloat16)
     flat_rows = normed.reshape(nchunk * row_count, model_width)
     row_total = nchunk * row_count
-    pieces = (
-        lax.all_gather(w_query, "queue", axis=0, tiled=True),
-        lax.all_gather(w_key, "queue", axis=0, tiled=True),
-        lax.all_gather(w_value, "queue", axis=0, tiled=True),
-    )
+    full_query, full_key, full_value, full_out = gather_weights(w_query, w_key, w_value, w_out.T)
+    pieces = (full_query, full_key, full_value)
     query, keyproj, valueproj = tuple(
         (
             jnp.dot(flat_rows, piece_rows, preferred_element_type=jnp.float32)
@@ -123,9 +262,10 @@
         "chqk,ckhd->cqhd", prob_bf, value_windows, preferred_element_type=jnp.float32
     )
     attended = attended.astype(jnp.bfloat16).reshape(row_total, local_cols)
-    partial_out = jnp.dot(
+    partial_out = lax.dot_general(
         attended,
-        lax.all_gather(w_out, "queue", axis=1, tiled=True),
+        full_out,
+        (((1,), (1,)), ((), ())),
         preferred_element_type=jnp.float32,
     )
     col_width = model_width // head_count

time: 835 us -> 472 us (0.57)
  waiting for transfers between devices: 682 us -> 119 us
  Pallas kernels: 0 us -> 185 us
    all_gather x4 -> x0, waiting for transfers between devices: 563 us -> none  [the longest x1 164 us: shards(): lax.all_gather(w_value, 'queue', axis=0, tiled=True)]
    pallas_call x0 -> x1, Pallas kernels: none -> 185 us  [gather_weights(): pl.pallas_call(gather_kernel, out_shape=[out] * 4, in_specs=[pl.BlockSpec...]
  transfers between devices with their start and end apart: 8 -> 4, of which waited for: 7 -> 4; matrix products, arithmetic and copies ran while one was open for 13% -> 5% of each run, Pallas kernels for 0% -> 0%
where the time goes in v1:
time: 472 us; the launch traced here: 464 us
  Pallas kernels  185 us (39%)
  waiting for transfers between devices  119 us (25%)
  matrix products  69.5 us (15%)
  other arithmetic  42 us (9%)
  local copies, waits for them, and re-layouts  17.4 us (4%)
  between operations  14.1 us (3%)
  blocking collectives  9.7 us (2%)
  starting transfers between devices  7.73 us (2%)
    pallas_call x1, Pallas kernels, gather_weights(): pl.pallas_call(gather_kernel, out_shape=[out] * 4, in_specs=[pl.BlockSpec...  185 us
    reduce_scatter x1, waiting for transfers between devices, shards(): lax.psum_scatter(partial_out.astype(jnp.bfloat16), 'head', scatter_dimens...  76.9 us
    dot_general x3, matrix products, shards(): jnp.dot(flat_rows, piece_rows, preferred_element_type=jnp.float32)  32.1 us
    ppermute x1, waiting for transfers between devices, shifted(): return lax.ppermute(value, axis, pairs)  26.8 us
    ppermute x2, waiting for transfers between devices, from_behind(): return lax.ppermute(value, axis, pairs)  15.5 us
    sub x1, matrix products, shards(): expo = jnp.exp(scores - top)  14.5 us
    add x1, other arithmetic, shards(): hidden = latents.astype(jnp.float32) + control.astype(jnp.float32)  13.6 us
    dot_general x1, matrix products, shards(): lax.dot_general(attended, full_out, (((1,), (1,)), ((), ())), preferred_e...  11.7 us
  transfers between devices with their start and end apart: 4, of which 4 were waited for; matrix products, arithmetic and copies ran while one was open for 5% of the time, Pallas kernels for 0%

profile of v1, /device:TPU:0, one launch (start us, length us, event | category | flops | bytes accessed | tf_op | source)
XLA Modules:
  0.0 464.4 jit_solution(15656615458162857268)
XLA Ops:
  6.5 3.5 fusion.6
  10.1 13.6 %convert_add_fusion = (f32[2,384,5120]{2,1,0:T(8,128)}, f32[2,384]{1,0:T(2,128)S(1)}) fusion(bf16[2,384,5120]{2,1,0:T(8,128)(2,1)} %param.12, bf16[2,384,5120]{2,1,0:T(8,128)(2,1)} %param.11), kind=kLoop, calls=%fused_computation.6 | loop fusion | flops 15727872 | bytes 31460352 | tf_op jit(solution)/shard_map/add | solution.py:203
  23.8 6.4 %multiply_reduce_fusion = f32[2,384]{1,0:T(2,128)S(1)} fusion(f32[2,384]{1,0:T(2,128)S(1)} %broadcast_multiply_fusion, bf16[2,384,5120]{2,1,0:T(8,128)(2,1)S(1)} %bitcast.59, bf16[2,384,5120]{2,1,0:T(8,128)(2,1)} %param.11), kind=kLoop, calls=%fused_computation.5 | loop fusion | flops 23592192 | bytes 15734784 | tf_op jit(solution)/shard_map/reduce_sum | solution.py:165
  30.2 9.4 %add_convert_fusion = bf16[2,384,5120]{2,1,0:T(8,128)(2,1)} fusion(f32[2,5120]{1,0:T(2,128)S(1)} %get-tuple-element.22, f32[2,5120]{1,0:T(2,128)S(1)} %get-tuple-element.23, f32[2,384]{1,0:T(2,128)S(1)} %add_rsqrt_fusion.2, f32[2,384]{1,0:T(2,128)S(1)} %broadcast_multiply_fusion, bf16[2,384,5120]{2,1,0:T(8,128)(2,1)S(1)} %bitcast.59, ...), kind=kLoop, calls=%fused_computation.4 | loop fusion | flops 31457280 | bytes 23681024 | tf_op jit(solution)/shard_map/convert_element_type | solution.py:212
  39.5 184.8 %gather_weights.1 = (bf16[5120,640]{1,0:T(8,128)(2,1)}, bf16[5120,640]{1,0:T(8,128)(2,1)}, bf16[5120,640]{1,0:T(8,128)(2,1)}, bf16[5120,640]{1,0:T(8,128)(2,1)}) custom-call(bf16[160,640]{1,0:T(8,128)(2,1)} %wq.1, bf16[160,640]{1,0:T(8,128)(2,1)} %wk.1, bf16[160,640]{1,0:T(8,128)(2,1)} %wv.1, bf16[160,640]{1,0:T(8,128)(2,1)} %bitcast.70), custom_call_target="tpu_custom_call" | custom-call | tf_op jit(solution)/shard_map/gather_weights/pallas_call | solution.py:132
  224.4 10.6 %fusion.17 = (f32[768]{0:T(1024)S(1)}, bf16[768,640]{0,1:T(8,128)(2,1)S(1)}) fusion(bf16[768,5120]{1,0:T(8,128)(2,1)} %bitcast.60, bf16[5120,640]{1,0:T(8,128)(2,1)} %get-tuple-element.10), kind=kOutput, calls=%fused_computation.30 | convolution fusion | flops 5035129856 | bytes 15404032 | tf_op jit(solution)/shard_map/dot_general | solution.py:219
  235.0 10.1 %fusion.20 = (f32[768]{0:T(1024)S(1)}, bf16[768,640]{1,0:T(8,128)(2,1)}) fusion(bf16[768,5120]{1,0:T(8,128)(2,1)S(1)} %bitcast.62, bf16[5120,640]{1,0:T(8,128)(2,1)} %get-tuple-element.11), kind=kOutput, calls=%fused_computation.33 | convolution fusion | flops 5035129856 | bytes 15404032 | tf_op jit(solution)/shard_map/dot_general | solution.py:219
  245.1 9.7 %all-reduce = (f32[768]{0:T(1024)S(1)}, f32[768]{0:T(1024)S(1)}) all-reduce(f32[768]{0:T(1024)S(1)} %get-tuple-element.26, f32[768]{0:T(1024)S(1)} %get-tuple-element.28), channel_id=1, replica_groups=mesh['queue'=32,'head'=4] {'head'}, use_global_device_ids=true, to_apply=%region_5.0 | all-reduce | flops 1536 | bytes 12288 | tf_op jit(solution)/shard_map/psum | solution.py:226
  256.3 3.9 collective-permute-start.1
  260.2 11.5 %convolution_convert_fusion.3 = bf16[768,640]{1,0:T(8,128)(2,1)} fusion(bf16[768,5120]{1,0:T(8,128)(2,1)} %bitcast.61, bf16[5120,640]{1,0:T(8,128)(2,1)} %get-tuple-element.9), kind=kOutput, calls=%fused_computation.48 | convolution fusion | flops 5033656320 | bytes 15400960 | tf_op jit(solution)/shard_map/dot_general | solution.py:219
  271.7 3.1 collective-permute-start
  276.6 4.7 %collective-permute-done.1 = bf16[768,640]{1,0:T(8,128)(2,1)} collective-permute-done((bf16[768,640]{1,0:T(8,128)(2,1)S(1)}, bf16[768,640]{1,0:T(8,128)(2,1)}, u32[]{:S(2)}, u32[]{:S(2)}) %collective-permute-start.1) | collective-permute-done | bytes 983072 | tf_op jit(solution)/shard_map/ppermute | solution.py:154
  285.5 3.6 copy.23
  289.1 10.8 %collective-permute-done = bf16[768,640]{1,0:T(8,128)(2,1)} collective-permute-done((bf16[768,640]{1,0:T(8,128)(2,1)}, bf16[768,640]{1,0:T(8,128)(2,1)}, u32[]{:S(2)}, u32[]{:S(2)}) %collective-permute-start) | collective-permute-done | bytes 983072 | tf_op jit(solution)/shard_map/ppermute | solution.py:154
  299.9 3.2 fusion.28
  303.1 3.6 copy.19
  306.7 2.2 copy.20
  311.9 14.5 %fusion.56 = (f32[2,5,384]{2,1,0:T(8,128)S(1)}, f32[2,5,384,1152]{3,2,1,0:T(8,128)}) fusion(pred[2,1152]{1,0:T(4,128)(4,1)S(1)} %bitcast.71, bf16[1,1152,5,128]{3,1,2,0:T(8,128)(2,1)} %copy.24, bf16[1,1152,5,128]{3,1,2,0:T(8,128)(2,1)} %copy.23, bf16[2,384,5,128]{1,0,3,2:T(2,128)(2,1)} %reshape.85), kind=kOutput, calls=%fused_computation.78 | convolution fusion | flops 1151632512 | bytes 21644544 | tf_op jit(solution)/shard_map/sub | solution.py:259
  326.5 7.7 %fusion.32 = bf16[2,384,5,128]{1,3,2,0:T(8,128)(2,1)S(1)} fusion(f32[2,5,384,1152]{3,2,1,0:T(8,128)} %get-tuple-element.31, f32[2,5,384]{2,1,0:T(8,128)S(1)} %get-tuple-element.30, bf16[1,1152,5,128]{1,3,2,0:T(8,128)(2,1)S(1)} %bitcast.68, bf16[1,1152,5,128]{1,3,2,0:T(8,128)(2,1)S(1)} %bitcast.67), kind=kOutput, calls=%fused_computation.49 | convolution fusion | flops 1143275520 | bytes 21642240 | tf_op jit(solution)/shard_map/chqk,ckhd->cqhd/dot_general | solution.py:261
  335.3 11.7 %convolution_convert_fusion = bf16[768,5120]{1,0:T(8,128)(2,1)} fusion(bf16[768,640]{0,1:T(8,128)(2,1)S(1)} %bitcast.69, bf16[5120,640]{1,0:T(8,128)(2,1)} %get-tuple-element.12), kind=kOutput, calls=%fused_computation.12 | convolution fusion | flops 5037096960 | bytes 15400960 | tf_op jit(solution)/shard_map/dot_general | solution.py:265
  347.1 76.9 %reduce-scatter.2.cloned.1.call-done = bf16[768,1280]{1,0:T(8,128)(2,1)} async-done(((bf16[768,5120]{1,0:T(8,128)(2,1)}), bf16[768,1280]{1,0:T(8,128)(2,1)}) %reduce-scatter.2.cloned.1.call-update) | async-done | bytes 1966096 | tf_op jit(solution)/shard_map/reduce_scatter | solution.py:275
  423.9 3.1 fusion.9
  428.0 26.8 %collective-permute-done.2 = bf16[384,1280]{1,0:T(8,128)(2,1)S(1)} collective-permute-done((bf16[384,1280]{1,0:T(8,128)(2,1)S(1)}, bf16[384,1280]{1,0:T(8,128)(2,1)S(1)}, u32[]{:S(2)}, u32[]{:S(2)}) %collective-permute-start.2) | collective-permute-done | bytes 983072 | tf_op jit(solution)/shard_map/ppermute | solution.py:160
  454.9 2.2 pad_maximum_fusion
  (45 shorter events, 12.8 us)
Async XLA Ops:
  6.5 417.4 %reduce-scatter.2.cloned.1.call-start = ((), (), s32[]{:S(2)}) async-start(), calls=%async_computation.1 | async-start | bytes 9830400 | tf_op jit(solution)/shard_map/reduce_scatter | solution.py:275
  10.0 13.7 %slice-start = ((s8[7864320]{0:T(1024)(128)(4,1)}), s8[4194304]{0:T(1024)(128)(4,1)S(1)}, s32[]{:S(2)}) async-start(s8[7864320]{0:T(1024)(128)(4,1)} %bitcast.58), calls=%async_computation.2 | async-start | bytes 8388608
  10.1 13.7 %slice-start.1 = ((s8[7864320]{0:T(1024)(128)(4,1)}), s8[3670016]{0:T(1024)(128)(4,1)S(1)}, s32[]{:S(2)}) async-start(s8[7864320]{0:T(1024)(128)(4,1)} %bitcast.58), calls=%async_computation.3 | async-start | bytes 7340032
  224.4 10.6 %copy-start = (bf16[2,384,5120]{2,1,0:T(8,128)(2,1)S(1)}, bf16[2,384,5120]{2,1,0:T(8,128)(2,1)}, u32[]{:S(2)}) copy-start(bf16[2,384,5120]{2,1,0:T(8,128)(2,1)} %add_convert_fusion) | copy-start | bytes 23592964
  235.0 19.8 %copy-start.4 = (f32[640]{0:T(1024)S(1)}, f32[640]{0:T(1024)}, u32[]{:S(2)}) copy-start(f32[640]{0:T(1024)} %param.21) | copy-start | bytes 7684
  256.3 15.4 %copy-start.1 = (bf16[768,640]{1,0:T(8,128)(2,1)}, bf16[768,640]{1,0:T(8,128)(2,1)S(1)}, u32[]{:S(2)}) copy-start(bf16[768,640]{1,0:T(8,128)(2,1)S(1)} %fusion.22) | copy-start | bytes 2949124
  256.3 25.1 %collective-permute-start.1 = (bf16[768,640]{1,0:T(8,128)(2,1)S(1)}, bf16[768,640]{1,0:T(8,128)(2,1)}, u32[]{:S(2)}, u32[]{:S(2)}) collective-permute-start(bf16[768,640]{1,0:T(8,128)(2,1)S(1)} %fusion.22), channel_id=1, source_target_pairs={{0,4},{4,8},{8,12},{12,16},{16,20},{20,24},{24,28},{28,32},{32,36}... | collective-permute-start | bytes 2949128 | tf_op jit(solution)/shard_map/ppermute | solution.py:154
  260.2 14.6 %copy-start.6 = (s32[2,2]{1,0:T(2,128)S(1)}, s32[2,2]{1,0:T(2,128)}, u32[]{:S(2)}) copy-start(s32[2,2]{1,0:T(2,128)} %param.14) | copy-start | bytes 52
  260.2 15.0 %copy-start.5 = (f32[640]{0:T(1024)S(1)}, f32[640]{0:T(1024)}, u32[]{:S(2)}) copy-start(f32[640]{0:T(1024)} %param.20) | copy-start | bytes 7684
  271.7 28.2 %collective-permute-start = (bf16[768,640]{1,0:T(8,128)(2,1)}, bf16[768,640]{1,0:T(8,128)(2,1)}, u32[]{:S(2)}, u32[]{:S(2)}) collective-permute-start(bf16[768,640]{1,0:T(8,128)(2,1)} %convolution_convert_fusion.3), channel_id=1, source_target_pairs={{0,4},{4,8},{8,12},{12,16},{16,20},{20,24},{24,28},{28,32},{32,36}... | collective-permute-start | bytes 2949128 | tf_op jit(solution)/shard_map/ppermute | solution.py:154
  311.9 14.6 %copy-start.2 = (bf16[1152,640]{0,1:T(8,128)(2,1)S(1)}, bf16[1152,640]{0,1:T(8,128)(2,1)}, u32[]{:S(2)}) copy-start(bf16[1152,640]{0,1:T(8,128)(2,1)} %copy.19) | copy-start | bytes 4423684
  311.9 14.6 %copy-start.3 = (bf16[1152,640]{0,1:T(8,128)(2,1)S(1)}, bf16[1152,640]{0,1:T(8,128)(2,1)}, u32[]{:S(2)}) copy-start(bf16[1152,640]{0,1:T(8,128)(2,1)} %copy.20) | copy-start | bytes 4423684
  427.1 27.6 %collective-permute-start.2 = (bf16[384,1280]{1,0:T(8,128)(2,1)S(1)}, bf16[384,1280]{1,0:T(8,128)(2,1)S(1)}, u32[]{:S(2)}, u32[]{:S(2)}) collective-permute-start(bf16[384,1280]{1,0:T(8,128)(2,1)S(1)} %fusion.35), channel_id=1, source_target_pairs={{0,4},{4,8},{8,12},{12,16},{16,20},{20,24},{24,28},{28,32},{32,36}... | collective-permute-start | bytes 2949128 | tf_op jit(solution)/shard_map/ppermute | solution.py:160
Sparse Core Ops, SparseCore 0:
  347.2 76.7 reduce-scatter.1

commit v2 on v0

v2 whole, which is shorter than its diff:
```python
import functools

import jax
import jax.numpy as jnp
from jax import lax
from jax.experimental import pallas as pl
from jax.experimental.pallas import tpu as pltpu
from jax.sharding import PartitionSpec as P

HD = 128
MESH = pl.DeviceIdType.MESH
BF = jnp.bfloat16
F32 = jnp.float32
XCS = (384, 256, 384)
TILE = 192
LNB = 64


def place(x, y, z, c):
    x, y, z = x % 4, y % 4, z % 4
    return ((y * 4 + x) * 2 + z % 2, (z // 2) * 2 + c)


def where_am_i():
    q = lax.axis_index("queue")
    h = lax.axis_index("head")
    return (q // 2) % 4, q // 8, (h // 2) * 2 + q % 2, h % 2


def remote(src, dst, ss, rs, dev):
    return pltpu.make_async_remote_copy(
        src_ref=src, dst_ref=dst, send_sem=ss, recv_sem=rs, device_id=dev, device_id_type=MESH
    )


def project_kernel(
    lat, ctl, mods, wk, wv, wq, bias,
    qo, ko, vo, pko, pvo, biaso,
    W, N, lstage, cstage, acc, sq, sqr,
    stsem, plsem, plrsem, asem, arsem, bsem, brsem, fsem, frsem,
    xsem, xrsem, ssem, srsem, ksem, krsem, bisem, birsem,
    *, compute=True,
):
    x, y, z, c = where_am_i()
    zl = z % 2
    zh = z // 2
    mine = place(x, y, z, c)
    partner = place(x, y, z, 1 - c)
    swapped = c != zl
    p = y * 4 + x
    pn = (p + 1) % 16
    pp = (p + 15) % 16
    nxt = place(pn % 4, pn // 4, z, 1 - c)
    prv = place(pp % 4, pp // 4, z, 1 - c)

    barrier = pltpu.get_barrier_semaphore()

    def greet(dev):
        pl.semaphore_signal(barrier, inc=1, device_id=dev, device_id_type=MESH)

    for d in (1, 2, 3):
        greet(place(x + d, y, z, c))
        greet(place(x, y + d, z, c))
        greet(place(x, y, z + d, c))
    greet(partner)

    @pl.when(c == 1)
    def _():
        greet(nxt)

    @pl.when(c == 0)
    def _():
        greet(prv)

    @pl.when(swapped)
    def _():
        greet(place(x, y, z + 1, 1 - c))
        greet(place(x, y, z + 3, 1 - c))

    pl.semaphore_wait(barrier, jnp.where(swapped, 13, 11))

    swap_dev = place(x, y, 2 * zh + c, 1 - c)
    ws = (wk, wv, wq)

    def slot(m):
        return W.at[m, y, x, zl]

    @pl.when(swapped)
    def _():
        for m in range(3):
            remote(ws[m], slot(m), plsem.at[m], plrsem.at[m], swap_dev).start()
        remote(bias, biaso, bisem, birsem, swap_dev).start()

    @pl.when(jnp.logical_not(swapped))
    def _():
        for m in range(3):
            pltpu.make_async_copy(ws[m], slot(m), plsem.at[m]).start()
        pltpu.make_async_copy(bias, biaso, bisem).start()

    n_chunks = jnp.where(swapped, 384 // LNB, 768 // LNB)
    row0 = jnp.where(swapped, zh * 384, 0)
    out0 = jnp.where(swapped, 768, 0)

    def stage(i, s):
        r = pl.multiple_of(row0 + i * LNB, LNB)
        return (
            pltpu.make_async_copy(lat.at[pl.ds(r, LNB)], lstage.at[s], stsem.at[0, s]),
            pltpu.make_async_copy(ctl.at[pl.ds(r, LNB)], cstage.at[s], stsem.at[1, s]),
        )

    for cp in stage(0, 0):
        cp.start()

    def piece(m, half, d, part):
        rows = slice(None) if part is None else pl.ds(part * 80, 80)
        if half == 0:
            return W.at[m, y, (x + 4 - d) % 4, c, rows, pl.ds(0, XCS[m])]
        return W.at[m, (y + 4 - d) % 4, x, c, rows, pl.ds(XCS[m], 640 - XCS[m])]

    def chunk(m, half, d, part=None):
        many = slice(None) if part is None else pl.ds(part * 2, 2)
        if half == 0:
            return W.at[m, (y + 4 - d) % 4, many, c, :, pl.ds(0, XCS[m])]
        return W.at[m, many, (x + 4 - d) % 4, c, :, pl.ds(XCS[m], 640 - XCS[m])]

    def along(axis, way):
        d = 1 if way == 0 else 3
        return place(x + d, y, z, c) if axis == 0 else place(x, y + d, z, c)

    def a_copy(m, half, way, part):
        ref = piece(m, half, 0, part)
        return remote(ref, ref, asem.at[m, half, way, part], arsem.at[m, half, way, part], along(half, way))

    def a_relay(m, half, way):
        ref = piece(m, half, 1 if way == 0 else 3, way)
        return remote(ref, ref, asem.at[m, half, way, 2], arsem.at[m, half, way, 2], along(half, way))

    def b_copy(m, half, way, part):
        ref = chunk(m, half, 0, part)
        return remote(ref, ref, bsem.at[m, half, way, part], brsem.at[m, half, way, part], along(1 - half, way))

    def b_relay(m, half, way):
        ref = chunk(m, half, 1 if way == 0 else 3, way)
        return remote(ref, ref, bsem.at[m, half, way, 2], brsem.at[m, half, way, 2], along(1 - half, way))

    def f_copy(m, half, d):
        ref = chunk(m, half, d)
        return remote(ref, ref, fsem.at[m, half, d], frsem.at[m, half, d], partner)

    def step_a1(m):
        @pl.when(swapped)
        def _():
            remote(ws[m], W.at[m, y, x, c], plsem.at[m], plrsem.at[m], swap_dev).wait()

        @pl.when(jnp.logical_not(swapped))
        def _():
            pltpu.make_async_copy(ws[m], slot(m), plsem.at[m]).wait()

        for part in (0, 1):
            for way in (0, 1):
                for half in (0, 1):
                    a_copy(m, half, way, part ^ way).start()

    def step_a2(m):
        for way in (0, 1):
            for half in (0, 1):
                a_copy(m, half, way, way).wait_recv()
                a_relay(m, half, way).start()

    def step_b1(m):
        for half in (0, 1):
            for way in (0, 1):
                a_copy(m, half, way, 1 - way).wait_recv()
                a_relay(m, half, way).wait_recv()
        for part in (0, 1):
            for way in (0, 1):
                for half in (0, 1):
                    b_copy(m, half, way, part ^ way).start()
        for half in (0, 1):
            f_copy(m, half, 0).start()

    def step_b2(m):
        for way in (0, 1):
            for half in (0, 1):
                b_copy(m, half, way, way).wait_recv()
                b_relay(m, half, way).start()

    def step_f(m):
        for half in (0, 1):
            for way in (0, 1):
                b_copy(m, half, way, 1 - way).wait_recv()
                f_copy(m, half, 1 if way == 0 else 3).start()

    def step_f2(m):
        for half in (0, 1):
            for way in (0, 1):
                b_relay(m, half, way).wait_recv()
            f_copy(m, half, 2).start()

    step_a1(0)

    def x_copy(i, by):
        src = N.at[pl.ds(pl.multiple_of(768 + i * LNB, LNB), LNB)]
        dst = N.at[pl.ds(pl.multiple_of(zh * 384 + i * LNB, LNB), LNB)]
        k = 0 if by == 1 else 1
        return remote(src, dst, xsem.at[k, i], xrsem.at[zh, i], place(x, y, z + by, 1 - c))

    def ln_rows(i, s):
        span = jnp.where(swapped, zh, (i * LNB) // 384)

        def body(j, carry):
            r = pl.multiple_of(j * 16, 16)
            hid = lstage[s, pl.ds(r, 16), :].astype(F32) + cstage[s, pl.ds(r, 16), :].astype(F32)
            cen = hid - jnp.mean(hid, axis=-1, keepdims=True)
            var = jnp.mean(cen * cen, axis=-1, keepdims=True)
            nrm = cen * lax.rsqrt(var + 1e-6) * (1.0 + mods[span, 1:2, :]) + mods[span, 0:1, :]
            N[pl.ds(pl.multiple_of(out0 + i * LNB + r, 16), 16), :] = nrm.astype(BF)
            return carry

        lax.fori_loop(0, LNB // 16, body, 0)

    def ln_step(i, carry):
        s = i % 2

        @pl.when(i + 1 < n_chunks)
        def _():
            for cp in stage(i + 1, 1 - s):
                cp.start()

        for cp in stage(i, s):
            cp.wait()
        ln_rows(i, s)

        @pl.when(swapped & (i > 0))
        def _():
            x_copy(i - 1, 1).start()
            x_copy(i - 1, 3).start()

        return carry

    part_chunks = n_chunks // 6
    weave = {0: (step_a1, 1), 1: (step_a2, 0), 2: (step_a1, 2), 3: (step_b1, 0), 4: (step_a2, 1), 5: (step_a2, 2)}
    for seg in range(6):
        lax.fori_loop(seg * part_chunks, (seg + 1) * part_chunks, ln_step, 0)
        fn, m = weave[seg]
        fn(m)

    @pl.when(swapped)
    def _():
        x_copy(384 // LNB - 1, 1).start()
        x_copy(384 // LNB - 1, 3).start()

    def rows_of(r):
        return [pl.ds(pl.multiple_of(s * 384 + r * (TILE // 2), TILE // 2), TILE // 2) for s in (0, 1)]

    def lhs(r, k0, kn):
        return jnp.concatenate([N[rs, pl.ds(k0, kn)] for rs in rows_of(r)], axis=0)

    def put(m, r, cols, val, first):
        for s, rs in enumerate(rows_of(r)):
            part = val[s * (TILE // 2):(s + 1) * (TILE // 2)]
            if first:
                acc[m, rs, cols] = part
            else:
                acc[m, rs, cols] += part

    def x_dot(m, d, r, first):
        yy = (y + 4 - d) % 4
        w = W[m, yy, :, :, :, 0:XCS[m]].reshape(1280, XCS[m])
        v = jnp.dot(lhs(r, pl.multiple_of(yy * 1280, 1280), 1280), w, preferred_element_type=F32)
        put(m, r, slice(0, XCS[m]), v, first)

    def y_dot(m, xp, r, first):
        v = None
        for yy in range(4):
            w = W[m, yy, pl.ds(2 * xp, 2), :, :, XCS[m]:640].reshape(640, 640 - XCS[m])
            t = jnp.dot(lhs(r, pl.multiple_of(yy * 1280 + xp * 640, 640), 640), w, preferred_element_type=F32)
            v = t if v is None else v + t
        put(m, r, slice(XCS[m], 640), v, first)

    def shared(m, half, d):
        f_copy(m, half, d).wait_recv()

    def rows_ready(r):
        @pl.when(swapped)
        def _():
            for span in (0, 1):
                lo = r * (TILE // 2) // LNB
                hi = -(-(r + 1) * (TILE // 2) // LNB)
                prev = -(-r * (TILE // 2) // LNB)
                for i in range(max(lo, prev), hi):
                    src = N.at[pl.ds(768 + i * LNB, LNB)]
                    dst = N.at[pl.ds(span * 384 + i * LNB, LNB)]
                    remote(src, dst, xsem.at[0, i], xrsem.at[span, i], partner).wait_recv()

    seen_rows = set()
    seen_w = set()

    def task(m, rlo, rhi):
        for r in range(rlo, rhi):
            if r not in seen_rows:
                seen_rows.add(r)
                rows_ready(r)
        fresh = m not in seen_w
        seen_w.add(m)
        for kind, d in (("x", 0), ("x", 1), ("x", 3), ("y", 0), ("x", 2), ("y", 1)):
            if fresh:
                if kind == "x":
                    shared(m, 0, d)
                    if d == 2:
                        shared(m, 1, 2)
                elif d == 0:
                    for dd in (0, 1, 3):
                        shared(m, 1, dd)
            if compute:
                def body(r, carry, kind=kind, d=d):
                    if kind == "x":
                        x_dot(m, d, r, d == 0)
                    else:
                        y_dot(m, x // 2 if d == 0 else 1 - x // 2, r, d == 0)
                    return carry

                lax.fori_loop(rlo, rhi, body, 0)
            if fresh and kind == "x" and d == 0:
                step_b2(m)
                if m < 2:
                    step_b1(m + 1)
                step_f(m)
            if fresh and kind == "x" and d == 3:
                step_f2(m)

    def row_sq(m, dst):
        for t in range(6):
            v = acc[m, pl.ds(t * 128, 128), :].astype(BF).astype(F32)
            s = jnp.sum(v * v, axis=-1, keepdims=True)
            wide = jnp.broadcast_to(s, (128, 128))
            sq[dst, :, pl.ds(t * 128, 128)] = jnp.transpose(wide)[0:8, :]

    def s_copy(k, d):
        return remote(
            sq.at[k], sqr.at[k, d - 1], ssem.at[k, d - 1], srsem.at[k, d - 1], place(x, y, z + d, c)
        )

    def normalize(k, m, gain, out):
        for d in (1, 2, 3):
            s_copy(k, d).wait_recv()
        tot = sq[k] + sqr[k, 0] + sqr[k, 1] + sqr[k, 2]
        scale = lax.rsqrt(tot / 2560.0 + 1e-6)
        for t in range(6):
            col = jnp.transpose(jnp.broadcast_to(scale[0:1, t * 128:(t + 1) * 128], (128, 128)))
            rs = pl.ds(t * 128, 128)
            v = acc[m, rs, :].astype(BF).astype(F32)
            out[rs, :] = (v * col[:, 0:1] * biaso[gain:gain + 1, 0:640]).astype(BF)

    task(0, 0, 2)
    task(0, 2, 3)
    task(1, 0, 3)
    task(0, 3, 4)
    @pl.when(swapped)
    def _():
        remote(bias, biaso, bisem, birsem, swap_dev).wait()

    @pl.when(jnp.logical_not(swapped))
    def _():
        pltpu.make_async_copy(bias, biaso, bisem).wait()

    row_sq(0, 0)
    for d in (1, 3, 2):
        s_copy(0, d).start()
    task(1, 3, 4)
    for t in range(6):
        rs = pl.ds(t * 128, 128)
        vo[rs, :] = acc[1, rs, :].astype(BF)
    normalize(0, 0, 17, ko)

    def k_copy(i, dev):
        return remote((ko, vo)[i], (pko, pvo)[i], ksem.at[i], krsem.at[i], dev)

    @pl.when(c == 0)
    def _():
        for i in (0, 1):
            k_copy(i, partner).start()

    @pl.when(c == 1)
    def _():
        for i in (0, 1):
            k_copy(i, nxt).start()

    task(2, 0, 4)
    row_sq(2, 1)
    for d in (1, 3, 2):
        s_copy(1, d).start()
    normalize(1, 2, 16, qo)

    for i in (0, 1):
        k_copy(i, partner).wait_recv()
        k_copy(i, partner).wait_send()
    for k in (0, 1):
        for d in (1, 2, 3):
            s_copy(k, d).wait_send()
    for m in range(3):
        for half in (0, 1):
            for way in (0, 1):
                for part in (0, 1):
                    a_copy(m, half, way, part).wait_send()
                    b_copy(m, half, way, part).wait_send()
                a_relay(m, half, way).wait_send()
                b_relay(m, half, way).wait_send()
            for d in range(4):
                f_copy(m, half, d).wait_send()

    @pl.when(swapped)
    def _():
        for i in range(384 // LNB):
            x_copy(i, 1).wait_send()
            x_copy(i, 3).wait_send()


def project(lat, ctl, mods, wk, wv, wq, bias, compute=True):
    o = jax.ShapeDtypeStruct((768, 640), BF)
    any_ = pl.BlockSpec(memory_space=pl.ANY)
    vm = pl.BlockSpec(memory_space=pltpu.VMEM)
    D = pltpu.SemaphoreType.DMA
    return pl.pallas_call(
        functools.partial(project_kernel, compute=compute),
        out_shape=[o] * 5 + [jax.ShapeDtypeStruct((24, 1152), F32)],
        in_specs=[any_, any_, vm, any_, any_, any_, any_],
        out_specs=[vm] * 6,
        scratch_shapes=[
            pltpu.VMEM((3, 4, 4, 2, 160, 640), BF),
            pltpu.VMEM((1152, 5120), BF),
            pltpu.VMEM((2, LNB, 5120), BF),
            pltpu.VMEM((2, LNB, 5120), BF),
            pltpu.VMEM((3, 768, 640), F32),
            pltpu.VMEM((2, 8, 768), F32),
            pltpu.VMEM((2, 3, 8, 768), F32),
            D((2, 2)), D((3,)), D((3,)),
            D((3, 2, 2, 3)), D((3, 2, 2, 3)), D((3, 2, 2, 3)), D((3, 2, 2, 3)), D((3, 2, 4)), D((3, 2, 4)),
            D((2, 384 // LNB)), D((2, 384 // LNB)), D((2, 3)), D((2, 3)), D((2,)), D((2,)), D, D,
        ],
        compiler_params=pltpu.CompilerParams(
            collective_id=0, has_side_effects=True, vmem_limit_bytes=61 * 2**20
        ),
        name="project",
    )(lat, ctl, mods, wk, wv, wq, bias)


def attend_kernel(q, k, v, pk, pv, bias, out):
    for s in (0, 1):
        qs = q[s * 384:(s + 1) * 384, :]
        if s == 0:
            keys = (pk[0:384, :], pk[384:768, :], k[0:384, :])
            vals = (pv[0:384, :], pv[384:768, :], v[0:384, :])
        else:
            keys = (pk[384:768, :], k[0:384, :], k[384:768, :])
            vals = (pv[384:768, :], v[0:384, :], v[384:768, :])
        kk = jnp.concatenate(keys, axis=0)
        vv = jnp.concatenate(vals, axis=0)
        for t in range(3):
            sc = lax.dot_general(qs[t * 128:(t + 1) * 128], kk, (((1,), (1,)), ((), ())), preferred_element_type=F32)
            sc = sc * HD ** -0.5 + bias[8 * s:8 * s + 1, :]
            top = jnp.max(sc, axis=-1, keepdims=True)
            ex = jnp.exp(sc - top)
            pr = (ex * (1.0 / jnp.sum(ex, axis=-1, keepdims=True))).astype(BF)
            o = jnp.dot(pr, vv, preferred_element_type=F32)
            out[pl.ds(s * 384 + t * 128, 128), :] = o.astype(BF)


def attend(q, k, v, pk, pv, bias):
    blk = pl.BlockSpec((768, 128), lambda i: (0, i))
    return pl.pallas_call(
        attend_kernel,
        grid=(5,),
        out_shape=jax.ShapeDtypeStruct((768, 640), BF),
        in_specs=[blk] * 5 + [pl.BlockSpec((24, 1152), lambda i: (0, 0))],
        out_specs=blk,
        name="attend",
    )(q, k, v, pk, pv, bias)


def out_kernel(
    att, wo, lat, ctl, gate, out,
    WO, AT, lbuf, cbuf,
    lsem, rsem, rrsem, asem, arsem, bsem, brsem, tsem, trsem, fsem, frsem,
):
    x, y, z, c = where_am_i()
    zl = z % 2
    h = lax.axis_index("head")
    partner = place(x, y, z, 1 - c)
    mine = c == zl
    barrier = pltpu.get_barrier_semaphore()

    def greet(dev):
        pl.semaphore_signal(barrier, inc=1, device_id=dev, device_id_type=MESH)

    def swapdev(t):
        return ((h * 4 + x) * 2 + t, y)

    for d in (1, 2, 3):
        greet(place(x + d, y, z, c))
        greet(place(x, y + d, z, c))
        greet(place(x, y, z + d, c))
    greet(partner)

    @pl.when(y != h)
    def _():
        greet(swapdev(0))
        greet(swapdev(1))

    @pl.when(y == h)
    def _():
        greet(swapdev(1 - zl))

    pl.semaphore_wait(barrier, jnp.where(y != h, 12, 11))

    spot = WO.at[h, x, zl]

    @pl.when(y != h)
    def _():
        for t in (0, 1):
            remote(wo, spot, rsem.at[t], rrsem.at[zl], swapdev(t)).start()

    @pl.when(y == h)
    def _():
        pltpu.make_async_copy(wo, spot, lsem.at[0]).start()
        remote(wo, spot, rsem.at[0], rrsem.at[zl], swapdev(1 - zl)).start()

    cols = pl.ds(pl.multiple_of(h * 1280, 1280), 1280)
    stage = (
        pltpu.make_async_copy(lat.at[:, cols], lbuf, lsem.at[1]),
        pltpu.make_async_copy(ctl.at[:, cols], cbuf, lsem.at[2]),
    )
    for cp in stage:
        cp.start()

    own = AT.at[z]

    def t_copy(d):
        return remote(att, own, tsem.at[d - 1], trsem.at[d - 1], place(x, y, z + d, c))

    @pl.when(mine)
    def _():
        pltpu.make_async_copy(att, own, lsem.at[3]).start()
        t_copy(2).start()

    @pl.when(jnp.logical_not(mine))
    def _():
        t_copy(1).start()
        t_copy(3).start()

    def pc(t):
        return WO.at[y, x, t]

    @pl.when(y != h)
    def _():
        for t in (0, 1):
            remote(wo, pc(t), rsem.at[t], rrsem.at[t], partner).wait_recv()

    @pl.when(y == h)
    def _():
        pltpu.make_async_copy(wo, spot, lsem.at[0]).wait()
        remote(wo, spot, rsem.at[0], rrsem.at[1 - zl], partner).wait_recv()

    def along(axis, way):
        d = 1 if way == 0 else 3
        return place(x + d, y, z, c) if axis == 0 else place(x, y + d, z, c)

    def piece(half, d, part):
        rows = pl.ds(part * 80, 80)
        if half == 0:
            return WO.at[y, (x + 4 - d) % 4, 0, rows]
        return WO.at[(y + 4 - d) % 4, x, 1, rows]

    def chunk(half, d, part):
        many = pl.ds(part * 2, 2)
        if half == 0:
            return WO.at[(y + 4 - d) % 4, many, 0]
        return WO.at[many, (x + 4 - d) % 4, 1]

    def a_copy(half, way, part):
        ref = piece(half, 0, part)
        return remote(ref, ref, asem.at[half, way, part], arsem.at[half, way, part], along(half, way))

    def a_relay(half, way):
        ref = piece(half, 1 if way == 0 else 3, way)
        return remote(ref, ref, asem.at[half, way, 2], arsem.at[half, way, 2], along(half, way))

    def b_copy(half, way, part):
        ref = chunk(half, 0, part)
        return remote(ref, ref, bsem.at[half, way, part], brsem.at[half, way, part], along(1 - half, way))

    def b_relay(half, way):
        ref = chunk(half, 1 if way == 0 else 3, way)
        return remote(ref, ref, bsem.at[half, way, 2], brsem.at[half, way, 2], along(1 - half, way))

    every = [(half, way) for half in (0, 1) for way in (0, 1)]
    for part in (0, 1):
        for half, way in every:
            a_copy(half, way, part ^ way).start()
    for half, way in every:
        a_copy(half, way, way).wait_recv()
        a_relay(half, way).start()
    for half, way in every:
        a_copy(half, way, 1 - way).wait_recv()
        a_relay(half, way).wait_recv()
    for part in (0, 1):
        for half, way in every:
            b_copy(half, way, part ^ way).start()

    def f_copy(g):
        ref = AT.at[g]
        return remote(ref, ref, fsem.at[g], frsem.at[g], partner)

    @pl.when(mine)
    def _():
        pltpu.make_async_copy(att, own, lsem.at[3]).wait()
        f_copy(z).start()

    for half, way in every:
        b_copy(half, way, way).wait_recv()
        b_relay(half, way).start()

    @pl.when(mine)
    def _():
        for d in (1, 3, 2):
            g = (z + 4 - d) % 4
            remote(att, AT.at[g], tsem.at[d - 1], trsem.at[d - 1], partner).wait_recv()
            f_copy(g).start()

    @pl.when(jnp.logical_not(mine))
    def _():
        for g in range(4):
            f_copy(g).wait_recv()

    for half, way in every:
        b_copy(half, way, 1 - way).wait_recv()
    for half, way in every:
        b_relay(half, way).wait_recv()
    for cp in stage:
        cp.wait()

    def rows_body(r, carry):
        rs = pl.ds(pl.multiple_of(r * 128, 128), 128)
        acc = None
        for g in range(4):
            t = lax.dot_general(
                AT[g, rs, :], WO[g].reshape(1280, 640), (((1,), (1,)), ((), ())), preferred_element_type=F32
            ).astype(BF).astype(F32)
            acc = t if acc is None else acc + t
        hid = lbuf[rs, :].astype(F32) + cbuf[rs, :].astype(F32)
        out[rs, :] = hid + gate[r // 3] * acc
        return carry

    lax.fori_loop(0, 6, rows_body, 0)

    for half, way in every:
        for part in (0, 1):
            a_copy(half, way, part).wait_send()
            b_copy(half, way, part).wait_send()
        a_relay(half, way).wait_send()
        b_relay(half, way).wait_send()

    @pl.when(y != h)
    def _():
        for t in (0, 1):
            remote(wo, spot, rsem.at[t], rrsem.at[zl], swapdev(t)).wait_send()

    @pl.when(y == h)
    def _():
        remote(wo, spot, rsem.at[0], rrsem.at[zl], swapdev(1 - zl)).wait_send()

    @pl.when(mine)
    def _():
        t_copy(2).wait_send()
        for g in range(4):
            f_copy(g).wait_send()

    @pl.when(jnp.logical_not(mine))
    def _():
        t_copy(1).wait_send()
        t_copy(3).wait_send()


def out_project(att, wo, lat, ctl, gate):
    any_ = pl.BlockSpec(memory_space=pl.ANY)
    vm = pl.BlockSpec(memory_space=pltpu.VMEM)
    D = pltpu.SemaphoreType.DMA
    return pl.pallas_call(
        out_kernel,
        out_shape=jax.ShapeDtypeStruct((768, 1280), F32),
        in_specs=[any_, any_, any_, any_, vm],
        out_specs=vm,
        scratch_shapes=[
            pltpu.VMEM((4, 4, 2, 160, 640), BF),
            pltpu.VMEM((4, 768, 640), BF),
            pltpu.VMEM((768, 1280), BF),
            pltpu.VMEM((768, 1280), BF),
            D((4,)), D((2,)), D((2,)),
            D((2, 2, 3)), D((2, 2, 3)), D((2, 2, 3)), D((2, 2, 3)),
            D((3,)), D((3,)), D((4,)), D((4,)),
        ],
        compiler_params=pltpu.CompilerParams(
            collective_id=1, has_side_effects=True, vmem_limit_bytes=40 * 2**20
        ),
        name="out_project",
    )(att, wo, lat, ctl, gate)


def shards(latents, control, levels, window_mask, modulation, w_query, w_key, w_value, w_out, q_gain, k_gain):
    owner = lax.axis_index("queue")
    head = lax.axis_index("head")
    lat = latents.reshape(768, 5120)
    ctl = control.reshape(768, 5120)
    mods = jnp.stack([lax.dynamic_index_in_dim(modulation, levels[s], 0, keepdims=False) for s in (0, 1)])
    gate = lax.dynamic_slice_in_dim(mods[:, 2:3], head * 1280, 1280, 2)
    ids = owner * 2 + jnp.arange(2, dtype=jnp.int32)
    seen = jnp.stack(
        [(window_mask[:, 0] == 1) & (ids >= 2), (window_mask[:, 1] == 1) & (ids >= 1), jnp.ones((2,), dtype=bool)],
        axis=1,
    )
    bias = jnp.where(jnp.repeat(seen, 384, axis=1), 0.0, -1e30).astype(F32)
    bias = jnp.broadcast_to(bias[:, None, :], (2, 8, 1152)).reshape(16, 1152)
    gains = jnp.pad(jnp.stack([q_gain, k_gain]), ((0, 6), (0, 512)))
    bias = jnp.concatenate([bias, gains], axis=0)
    q, k, v, pk, pv, bias = project(
        lat, ctl, mods[:, 0:2], w_key, w_value, w_query, bias
    )
    att = attend(q, k, v, pk, pv, bias)
    updated = out_project(att, w_out.T, lat, ctl, gate)
    pairs = [(i, (i + 1) % 32) for i in range(32)]
    last = lax.ppermute(updated[384:].astype(BF), "queue", pairs).astype(F32)
    return jnp.stack([last, updated[:384]])


def solution(mesh):
    placed = (
        P("queue", None, None),
        P("queue", None, None),
        P("queue"),
        P("queue", None),
        P(),
        P("queue", "head"),
        P("queue", "head"),
        P("queue", "head"),
        P("head", "queue"),
        P("head"),
        P("head"),
    )
    return jax.shard_map(
        shards, mesh=mesh, in_specs=placed, out_specs=P("queue", None, "head"), check_vma=False
    )
```

time: 835 us -> 248 us (0.30)
  waiting for transfers between devices: 682 us -> 21.7 us
  Pallas kernels: 0 us -> 203 us
  matrix products: 69.5 us -> 0 us
  other arithmetic: 41.2 us -> 3.88 us
  between operations: 13.4 us -> 3.71 us
    all_gather x4 -> x0, waiting for transfers between devices: 563 us -> none  [the longest x1 164 us: shards(): lax.all_gather(w_value, 'queue', axis=0, tiled=True)]
    pallas_call x0 -> x3, Pallas kernels: none -> 203 us  [the longest x1 120 us: project(): pl.pallas_call(functools.partial(project_kernel, compute=compute), out_sh...]
    reduce_scatter x1 -> x0, waiting for transfers between devices: 76.6 us -> none  [shards(): lax.psum_scatter(partial_out.astype(jnp.bfloat16), 'head', scatter_dimens...]
    dot_general x6 -> x0, matrix products: 55 us -> none  [the longest x3 32.4 us: shards(): jnp.dot(flat_rows, piece_rows, preferred_element_type=jnp.float32)]
    ppermute x3 -> x1, waiting for transfers between devices: 39.3 us -> 21.7 us  [shards(): last = lax.ppermute(updated[384:].astype(BF), 'queue', pairs).astype(F32)]
    add x2 -> x0, other arithmetic: 16.8 us -> none  [the longest x1 13.7 us: shards(): hidden = latents.astype(jnp.float32) + control.astype(jnp.float32)]
    sub x1 -> x0, matrix products: 14.5 us -> none  [shards(): expo = jnp.exp(scores - top)]
    convert_element_type x3 -> x0, other arithmetic: 11.4 us -> none  [the longest x1 10.8 us: shards(): normed = (layer_norm(hidden) * (1.0 + level_mods[:, 1][:, None, :]) + lev...]
  transfers between devices with their start and end apart: 8 -> 1, of which waited for: 7 -> 1; matrix products, arithmetic and copies ran while one was open for 13% -> 0% of each run, Pallas kernels for 0% -> 0%
where the time goes in v2:
time: 248 us; the launch traced here: 245 us
  Pallas kernels  203 us (82%)
  waiting for transfers between devices  21.7 us (9%)
  local copies, waits for them, and re-layouts  9.56 us (4%)
  other arithmetic  3.88 us (2%)
  between operations  3.71 us (1%)
  starting transfers between devices  2.9 us (1%)
    pallas_call x1, Pallas kernels, project(): pl.pallas_call(functools.partial(project_kernel, compute=compute), out_sh...  120 us
    pallas_call x1, Pallas kernels, out_project(): pl.pallas_call(out_kernel, out_shape=jax.ShapeDtypeStruct((768, 1280), F3...  65.4 us
    ppermute x1, waiting for transfers between devices, shards(): last = lax.ppermute(updated[384:].astype(BF), 'queue', pairs).astype(F32)  21.7 us
    pallas_call x1, Pallas kernels, attend(): pl.pallas_call(attend_kernel, grid=(5,), out_shape=jax.ShapeDtypeStruct((...  18 us
  transfers between devices with their start and end apart: 1, of which 1 were waited for; matrix products, arithmetic and copies ran while one was open for 0% of the time, Pallas kernels for 0%

profile of v2, /device:TPU:0, one launch (start us, length us, event | category | flops | bytes accessed | tf_op | source)
XLA Modules:
  0.0 245.2 jit_solution(3900283920282001436)
XLA Ops:
  0.0 1.3 fusion
  4.9 1.3 constant_dynamic-slice_fusion.1
  6.3 0.7 slice.33.mods
  7.0 0.7 stack.33
  7.7 0.7 stack.34
  8.4 0.1 pad.13.clone
  8.4 0.8 compare_and_fusion.1
  9.3 0.1 add_select_fusion
  9.4 0.1 broadcast_bitcast_fusion.1
  9.5 0.7 pad_maximum_fusion.1.bias
  10.1 120.1 %project.1 = (bf16[768,640]{1,0:T(8,128)(2,1)}, bf16[768,640]{1,0:T(8,128)(2,1)}, bf16[768,640]{1,0:T(8,128)(2,1)}, bf16[768,640]{1,0:T(8,128)(2,1)}, bf16[768,640]{1,0:T(8,128)(2,1)}, /*index=5*/f32[24,1152]{1,0:T(8,128)}) custom-call(bf16[768,5120]{1,0:T(8,128)(2,1)} %bitcast.16, bf16[768,5120]{1,0:T(8,128)(2,1)} %bitcast.19, f32[2,2,5120]{2,1,0:T(2,128)} %slice.33.mods, ...), custom_call_target="tpu_custom_call" | custom-call | tf_op jit(solution)/shard_map/project/pallas_call | solution.py:424
  130.2 0.0 copy-start.2
  130.2 18.0 %attend.1.att = bf16[768,640]{1,0:T(8,128)(2,1)} custom-call(bf16[768,640]{1,0:T(8,128)(2,1)} %get-tuple-element.11.q, bf16[768,640]{1,0:T(8,128)(2,1)} %get-tuple-element.12.k, bf16[768,640]{1,0:T(8,128)(2,1)} %get-tuple-element.13.v, bf16[768,640]{1,0:T(8,128)(2,1)} %get-tuple-element.14.pk, bf16[768,640]{1,0:T(8,128)(2,1)} %get-tuple-element.15.pv, ...), custom_call_target="tpu_custom_call" | custom-call | tf_op jit(solution)/shard_map/attend/pallas_call | solution.py:471
  148.3 0.0 copy-done.2
  148.3 0.0 copy-start
  148.3 3.2 %copy-done = bf16[2,384,5120]{2,1,0:T(8,128)(2,1)S(1)} copy-done((bf16[2,384,5120]{2,1,0:T(8,128)(2,1)S(1)}, bf16[2,384,5120]{2,1,0:T(8,128)(2,1)}, u32[]{:S(2)}) %copy-start) | copy-done | bytes 7864344
  151.5 1.2 copy-done.1
  152.7 65.4 %out_project.1 = f32[768,1280]{1,0:T(8,128)S(1)} custom-call(bf16[768,640]{1,0:T(8,128)(2,1)S(1)} %copy-done.1, bf16[160,640]{1,0:T(8,128)(2,1)S(1)} %bitcast.18, bf16[768,5120]{1,0:T(8,128)(2,1)S(1)} %bitcast.17, bf16[768,5120]{1,0:T(8,128)(2,1)} %bitcast.20, f32[2,1,1280]{2,1,0:T(1,128)S(1)} %constant_dynamic-slice_fusion.gate), custom_call_target="tpu_custom_call" | custom-call | tf_op jit(solution)/shard_map/out_project/pallas_call | solution.py:688
  218.1 0.1 slice.40
  218.2 2.9 %collective-permute-start = (bf16[384,1280]{1,0:T(8,128)(2,1)S(1)}, bf16[384,1280]{1,0:T(8,128)(2,1)S(1)}, u32[]{:S(2)}, u32[]{:S(2)}) collective-permute-start(bf16[384,1280]{1,0:T(8,128)(2,1)S(1)} %slice.40), channel_id=1, source_target_pairs={{0,4},{4,8},{8,12},{12,16},{16,20},{20,24},{24,28},{28,32},{32,36}... | collective-permute-start | bytes 2949128 | tf_op jit(solution)/shard_map/ppermute | solution.py:731
  221.1 0.1 slice_bitcast_fusion
  221.2 21.7 %collective-permute-done = bf16[384,1280]{1,0:T(8,128)(2,1)S(1)} collective-permute-done((bf16[384,1280]{1,0:T(8,128)(2,1)S(1)}, bf16[384,1280]{1,0:T(8,128)(2,1)S(1)}, u32[]{:S(2)}, u32[]{:S(2)}) %collective-permute-start) | collective-permute-done | bytes 983072 | tf_op jit(solution)/shard_map/ppermute | solution.py:731
  242.9 0.1 bitcast_convert_fusion
  243.0 2.2 pad_maximum_fusion
  (8 shorter events, 0.1 us)
Async XLA Ops:
  130.2 18.0 %copy-start.2 = (bf16[640,160]{0,1:T(8,128)(2,1)S(1)}, bf16[640,160]{0,1:T(8,128)(2,1)}, u32[]{:S(2)}) copy-start(bf16[640,160]{0,1:T(8,128)(2,1)} %param.19) | copy-start | bytes 614404
  148.3 3.2 %copy-start = (bf16[2,384,5120]{2,1,0:T(8,128)(2,1)S(1)}, bf16[2,384,5120]{2,1,0:T(8,128)(2,1)}, u32[]{:S(2)}) copy-start(bf16[2,384,5120]{2,1,0:T(8,128)(2,1)} %param.11) | copy-start | bytes 23592964
  151.5 1.2 copy-start.1
  218.2 24.7 %collective-permute-start = (bf16[384,1280]{1,0:T(8,128)(2,1)S(1)}, bf16[384,1280]{1,0:T(8,128)(2,1)S(1)}, u32[]{:S(2)}, u32[]{:S(2)}) collective-permute-start(bf16[384,1280]{1,0:T(8,128)(2,1)S(1)} %slice.40), channel_id=1, source_target_pairs={{0,4},{4,8},{8,12},{12,16},{16,20},{20,24},{24,28},{28,32},{32,36}... | collective-permute-start | bytes 2949128 | tf_op jit(solution)/shard_map/ppermute | solution.py:731

commit v3 on v2

v3 whole, which is shorter than its diff:
```python
import functools

import jax
import jax.numpy as jnp
from jax import lax
from jax.experimental import pallas as pl
from jax.experimental.pallas import tpu as pltpu
from jax.sharding import PartitionSpec as P

HD = 128
MESH = pl.DeviceIdType.MESH
BF = jnp.bfloat16
F32 = jnp.float32
XCS = (384, 256, 384)
TILE = 192
LNB = 64


def place(x, y, z, c):
    x, y, z = x % 4, y % 4, z % 4
    return ((y * 4 + x) * 2 + z % 2, (z // 2) * 2 + c)


def where_am_i():
    q = lax.axis_index("queue")
    h = lax.axis_index("head")
    return (q // 2) % 4, q // 8, (h // 2) * 2 + q % 2, h % 2


def remote(src, dst, ss, rs, dev):
    return pltpu.make_async_remote_copy(
        src_ref=src, dst_ref=dst, send_sem=ss, recv_sem=rs, device_id=dev, device_id_type=MESH
    )


def block_kernel(
    lat, ctl, mods, wk, wv, wq, bias, wo, gate,
    out,
    W, N, lstage, cstage, acc, sq, sqr, qo, ko, vo, pko, pvo, biaso, WO, AT, shout, shin,
    stsem, plsem, plrsem, asem, arsem, bsem, brsem, fsem, frsem,
    xsem, xrsem, ssem, srsem, ksem, krsem, bisem, birsem,
    rsem, rrsem, wasem, warsem, wbsem, wbrsem, tsem, trsem, gsem, grsem, lsem, hsem, hrsem,
):
    x, y, z, c = where_am_i()
    zl = z % 2
    zh = z // 2
    mine = place(x, y, z, c)
    partner = place(x, y, z, 1 - c)
    swapped = c != zl
    p = y * 4 + x
    pn = (p + 1) % 16
    pp = (p + 15) % 16
    nxt = place(pn % 4, pn // 4, z, 1 - c)
    prv = place(pp % 4, pp // 4, z, 1 - c)

    q = lax.axis_index("queue")
    h = lax.axis_index("head")
    after = ((q + 1) % 32, h)
    before = ((q + 31) % 32, h)
    barrier = pltpu.get_barrier_semaphore()

    def swapdev(t):
        return ((h * 4 + x) * 2 + t, y)


    def greet(dev):
        pl.semaphore_signal(barrier, inc=1, device_id=dev, device_id_type=MESH)

    for d in (1, 2, 3):
        greet(place(x + d, y, z, c))
        greet(place(x, y + d, z, c))
        greet(place(x, y, z + d, c))
    greet(partner)

    @pl.when(c == 1)
    def _():
        greet(nxt)

    @pl.when(c == 0)
    def _():
        greet(prv)

    @pl.when(swapped)
    def _():
        greet(place(x, y, z + 1, 1 - c))
        greet(place(x, y, z + 3, 1 - c))

    @pl.when(y != h)
    def _():
        greet(swapdev(0))
        greet(swapdev(1))

    @pl.when(y == h)
    def _():
        greet(swapdev(1 - zl))

    greet(after)
    greet(before)
    pl.semaphore_wait(barrier, jnp.where(swapped, 13, 11) + jnp.where(y != h, 2, 1) + 2)

    swap_dev = place(x, y, 2 * zh + c, 1 - c)
    ws = (wk, wv, wq)

    def slot(m):
        return W.at[m, y, x, zl]

    @pl.when(swapped)
    def _():
        for m in range(3):
            remote(ws[m], slot(m), plsem.at[m], plrsem.at[m], swap_dev).start()
        remote(bias, biaso, bisem, birsem, swap_dev).start()

    @pl.when(jnp.logical_not(swapped))
    def _():
        for m in range(3):
            pltpu.make_async_copy(ws[m], slot(m), plsem.at[m]).start()
        pltpu.make_async_copy(bias, biaso, bisem).start()

    n_chunks = jnp.where(swapped, 384 // LNB, 768 // LNB)
    row0 = jnp.where(swapped, zh * 384, 0)
    out0 = jnp.where(swapped, 768, 0)

    def stage(i, s):
        r = pl.multiple_of(row0 + i * LNB, LNB)
        return (
            pltpu.make_async_copy(lat.at[pl.ds(r, LNB)], lstage.at[s], stsem.at[0, s]),
            pltpu.make_async_copy(ctl.at[pl.ds(r, LNB)], cstage.at[s], stsem.at[1, s]),
        )

    for cp in stage(0, 0):
        cp.start()

    def piece(m, half, d, part):
        rows = slice(None) if part is None else pl.ds(part * 80, 80)
        if half == 0:
            return W.at[m, y, (x + 4 - d) % 4, c, rows, pl.ds(0, XCS[m])]
        return W.at[m, (y + 4 - d) % 4, x, c, rows, pl.ds(XCS[m], 640 - XCS[m])]

    def chunk(m, half, d, part=None):
        many = slice(None) if part is None else pl.ds(part * 2, 2)
        if half == 0:
            return W.at[m, (y + 4 - d) % 4, many, c, :, pl.ds(0, XCS[m])]
        return W.at[m, many, (x + 4 - d) % 4, c, :, pl.ds(XCS[m], 640 - XCS[m])]

    def along(axis, way):
        d = 1 if way == 0 else 3
        return place(x + d, y, z, c) if axis == 0 else place(x, y + d, z, c)

    def a_copy(m, half, way, part):
        ref = piece(m, half, 0, part)
        return remote(ref, ref, asem.at[m, half, way, part], arsem.at[m, half, way, part], along(half, way))

    def a_relay(m, half, way):
        ref = piece(m, half, 1 if way == 0 else 3, way)
        return remote(ref, ref, asem.at[m, half, way, 2], arsem.at[m, half, way, 2], along(half, way))

    def b_copy(m, half, way, part):
        ref = chunk(m, half, 0, part)
        return remote(ref, ref, bsem.at[m, half, way, part], brsem.at[m, half, way, part], along(1 - half, way))

    def b_relay(m, half, way):
        ref = chunk(m, half, 1 if way == 0 else 3, way)
        return remote(ref, ref, bsem.at[m, half, way, 2], brsem.at[m, half, way, 2], along(1 - half, way))

    def f_copy(m, half, d):
        ref = chunk(m, half, d)
        return remote(ref, ref, fsem.at[m, half, d], frsem.at[m, half, d], partner)

    def step_a1(m):
        @pl.when(swapped)
        def _():
            remote(ws[m], W.at[m, y, x, c], plsem.at[m], plrsem.at[m], swap_dev).wait()

        @pl.when(jnp.logical_not(swapped))
        def _():
            pltpu.make_async_copy(ws[m], slot(m), plsem.at[m]).wait()

        for part in (0, 1):
            for way in (0, 1):
                for half in (0, 1):
                    a_copy(m, half, way, part ^ way).start()

    def step_a2(m):
        for way in (0, 1):
            for half in (0, 1):
                a_copy(m, half, way, way).wait_recv()
                a_relay(m, half, way).start()

    def step_b1(m):
        for half in (0, 1):
            for way in (0, 1):
                a_copy(m, half, way, 1 - way).wait_recv()
                a_relay(m, half, way).wait_recv()
        for part in (0, 1):
            for way in (0, 1):
                for half in (0, 1):
                    b_copy(m, half, way, part ^ way).start()
        for half in (0, 1):
            f_copy(m, half, 0).start()

    def step_b2(m):
        for way in (0, 1):
            for half in (0, 1):
                b_copy(m, half, way, way).wait_recv()
                b_relay(m, half, way).start()

    def step_f(m):
        for half in (0, 1):
            for way in (0, 1):
                b_copy(m, half, way, 1 - way).wait_recv()
                f_copy(m, half, 1 if way == 0 else 3).start()

    def step_f2(m):
        for half in (0, 1):
            for way in (0, 1):
                b_relay(m, half, way).wait_recv()
            f_copy(m, half, 2).start()

    step_a1(0)

    def x_copy(i, by):
        src = N.at[pl.ds(pl.multiple_of(768 + i * LNB, LNB), LNB)]
        dst = N.at[pl.ds(pl.multiple_of(zh * 384 + i * LNB, LNB), LNB)]
        k = 0 if by == 1 else 1
        return remote(src, dst, xsem.at[k, i], xrsem.at[zh, i], place(x, y, z + by, 1 - c))

    def ln_rows(i, s):
        span = jnp.where(swapped, zh, (i * LNB) // 384)

        def body(j, carry):
            r = pl.multiple_of(j * 16, 16)
            hid = lstage[s, pl.ds(r, 16), :].astype(F32) + cstage[s, pl.ds(r, 16), :].astype(F32)
            cen = hid - jnp.mean(hid, axis=-1, keepdims=True)
            var = jnp.mean(cen * cen, axis=-1, keepdims=True)
            nrm = cen * lax.rsqrt(var + 1e-6) * (1.0 + mods[span, 1:2, :]) + mods[span, 0:1, :]
            N[pl.ds(pl.multiple_of(out0 + i * LNB + r, 16), 16), :] = nrm.astype(BF)
            return carry

        lax.fori_loop(0, LNB // 16, body, 0)

    def ln_step(i, carry):
        s = i % 2

        @pl.when(i + 1 < n_chunks)
        def _():
            for cp in stage(i + 1, 1 - s):
                cp.start()

        for cp in stage(i, s):
            cp.wait()
        ln_rows(i, s)

        @pl.when(swapped & (i > 0))
        def _():
            x_copy(i - 1, 1).start()
            x_copy(i - 1, 3).start()

        return carry

    part_chunks = n_chunks // 6
    weave = {0: (step_a1, 1), 1: (step_a2, 0), 2: (step_a1, 2), 3: (step_b1, 0), 4: (step_a2, 1), 5: (step_a2, 2)}
    for seg in range(6):
        lax.fori_loop(seg * part_chunks, (seg + 1) * part_chunks, ln_step, 0)
        fn, m = weave[seg]
        fn(m)

    @pl.when(swapped)
    def _():
        x_copy(384 // LNB - 1, 1).start()
        x_copy(384 // LNB - 1, 3).start()

    def rows_of(r):
        return [pl.ds(pl.multiple_of(s * 384 + r * (TILE // 2), TILE // 2), TILE // 2) for s in (0, 1)]

    def lhs(r, k0, kn):
        return jnp.concatenate([N[rs, pl.ds(k0, kn)] for rs in rows_of(r)], axis=0)

    def put(m, r, cols, val, first):
        for s, rs in enumerate(rows_of(r)):
            part = val[s * (TILE // 2):(s + 1) * (TILE // 2)]
            if first:
                acc[m, rs, cols] = part
            else:
                acc[m, rs, cols] += part

    def x_dot(m, d, r, first):
        yy = (y + 4 - d) % 4
        w = W[m, yy, :, :, :, 0:XCS[m]].reshape(1280, XCS[m])
        v = jnp.dot(lhs(r, pl.multiple_of(yy * 1280, 1280), 1280), w, preferred_element_type=F32)
        put(m, r, slice(0, XCS[m]), v, first)

    def y_dot(m, xp, r, first):
        v = None
        for yy in range(4):
            w = W[m, yy, pl.ds(2 * xp, 2), :, :, XCS[m]:640].reshape(640, 640 - XCS[m])
            t = jnp.dot(lhs(r, pl.multiple_of(yy * 1280 + xp * 640, 640), 640), w, preferred_element_type=F32)
            v = t if v is None else v + t
        put(m, r, slice(XCS[m], 640), v, first)

    def shared(m, half, d):
        f_copy(m, half, d).wait_recv()

    def rows_ready(r):
        @pl.when(swapped)
        def _():
            for span in (0, 1):
                lo = r * (TILE // 2) // LNB
                hi = -(-(r + 1) * (TILE // 2) // LNB)
                prev = -(-r * (TILE // 2) // LNB)
                for i in range(max(lo, prev), hi):
                    src = N.at[pl.ds(768 + i * LNB, LNB)]
                    dst = N.at[pl.ds(span * 384 + i * LNB, LNB)]
                    remote(src, dst, xsem.at[0, i], xrsem.at[span, i], partner).wait_recv()

    def row_sq(m, dst):
        for t in range(6):
            v = acc[m, pl.ds(t * 128, 128), :].astype(BF).astype(F32)
            s = jnp.sum(v * v, axis=-1, keepdims=True)
            wide = jnp.broadcast_to(s, (128, 128))
            sq[dst, :, pl.ds(t * 128, 128)] = jnp.transpose(wide)[0:8, :]

    def s_copy(k, d):
        return remote(
            sq.at[k], sqr.at[k, d - 1], ssem.at[k, d - 1], srsem.at[k, d - 1], place(x, y, z + d, c)
        )

    def normalize(k, m, gain, out):
        for d in (1, 2, 3):
            s_copy(k, d).wait_recv()
        tot = sq[k] + sqr[k, 0] + sqr[k, 1] + sqr[k, 2]
        scale = lax.rsqrt(tot / 2560.0 + 1e-6)
        for t in range(6):
            col = jnp.transpose(jnp.broadcast_to(scale[0:1, t * 128:(t + 1) * 128], (128, 128)))
            rs = pl.ds(t * 128, 128)
            v = acc[m, rs, :].astype(BF).astype(F32)
            out[rs, :] = (v * col[:, 0:1] * biaso[gain:gain + 1, 0:640]).astype(BF)

    def steps(m, kinds, rlo, rhi, fresh):
        for kind, d in kinds:
            if fresh:
                if kind == "x":
                    shared(m, 0, d)
                elif d == 0:
                    for dd in (0, 1, 3):
                        shared(m, 1, dd)
                else:
                    shared(m, 1, 2)

            def body(r, carry, kind=kind, d=d):
                if kind == "x":
                    x_dot(m, d, r, d == 0)
                else:
                    y_dot(m, x // 2 if d == 0 else 1 - x // 2, r, d == 0)
                return carry

            lax.fori_loop(rlo, rhi, body, 0)

    early = (("x", 0), ("x", 1), ("x", 3), ("y", 0))
    late = (("x", 2), ("y", 1))

    spot = WO.at[h, x, zl]

    def w_place():
        @pl.when(y != h)
        def _():
            for t in (0, 1):
                remote(wo, spot, rsem.at[t], rrsem.at[zl], swapdev(t)).start()

        @pl.when(y == h)
        def _():
            pltpu.make_async_copy(wo, spot, lsem.at[0]).start()
            remote(wo, spot, rsem.at[0], rrsem.at[zl], swapdev(1 - zl)).start()

    def w_placed():
        @pl.when(y != h)
        def _():
            for t in (0, 1):
                remote(wo, WO.at[y, x, t], rsem.at[t], rrsem.at[t], partner).wait_recv()

        @pl.when(y == h)
        def _():
            pltpu.make_async_copy(wo, spot, lsem.at[0]).wait()
            remote(wo, spot, rsem.at[0], rrsem.at[1 - zl], partner).wait_recv()

    def w_piece(half, d, part):
        rows = pl.ds(part * 80, 80)
        if half == 0:
            return WO.at[y, (x + 4 - d) % 4, 0, rows]
        return WO.at[(y + 4 - d) % 4, x, 1, rows]

    def w_chunk(half, d, part):
        many = pl.ds(part * 2, 2)
        if half == 0:
            return WO.at[(y + 4 - d) % 4, many, 0]
        return WO.at[many, (x + 4 - d) % 4, 1]

    def wa_copy(half, way, part):
        ref = w_piece(half, 0, part)
        return remote(ref, ref, wasem.at[half, way, part], warsem.at[half, way, part], along(half, way))

    def wa_relay(half, way):
        ref = w_piece(half, 1 if way == 0 else 3, way)
        return remote(ref, ref, wasem.at[half, way, 2], warsem.at[half, way, 2], along(half, way))

    def wb_copy(half, way, part):
        ref = w_chunk(half, 0, part)
        return remote(ref, ref, wbsem.at[half, way, part], wbrsem.at[half, way, part], along(1 - half, way))

    def wb_relay(half, way):
        ref = w_chunk(half, 1 if way == 0 else 3, way)
        return remote(ref, ref, wbsem.at[half, way, 2], wbrsem.at[half, way, 2], along(1 - half, way))

    every = [(half, way) for way in (0, 1) for half in (0, 1)]

    def w_a1():
        w_placed()
        for part in (0, 1):
            for half, way in every:
                wa_copy(half, way, part ^ way).start()

    def w_a2():
        for half, way in every:
            wa_copy(half, way, way).wait_recv()
            wa_relay(half, way).start()

    def w_b1():
        for half, way in every:
            wa_copy(half, way, 1 - way).wait_recv()
            wa_relay(half, way).wait_recv()
        for part in (0, 1):
            for half, way in every:
                wb_copy(half, way, part ^ way).start()

    def w_b2():
        for half, way in every:
            wb_copy(half, way, way).wait_recv()
            wb_relay(half, way).start()

    def w_done():
        for half, way in every:
            wb_copy(half, way, 1 - way).wait_recv()
        for half, way in every:
            wb_relay(half, way).wait_recv()

    def head_cols(i):
        return pl.ds(i * HD, HD)

    def k_copy(t, i, dev):
        return remote(
            (ko, vo)[t].at[:, head_cols(i)], (pko, pvo)[t].at[:, head_cols(i)], ksem.at[t, i], krsem.at[t, i], dev
        )

    w_place()
    step_b2(0)
    step_b1(1)
    step_f(0)
    step_f2(0)
    rows_ready(0)
    rows_ready(1)
    steps(0, early + late, 0, 2, True)
    step_b2(1)
    step_b1(2)
    step_f(1)
    rows_ready(2)
    steps(0, early + late, 2, 3, False)
    step_f2(1)
    steps(1, early + late, 0, 3, True)
    step_b2(2)
    step_f(2)
    w_a1()
    rows_ready(3)
    steps(0, early + late, 3, 4, False)

    @pl.when(swapped)
    def _():
        remote(bias, biaso, bisem, birsem, swap_dev).wait()

    @pl.when(jnp.logical_not(swapped))
    def _():
        pltpu.make_async_copy(bias, biaso, bisem).wait()

    row_sq(0, 0)
    for d in (1, 3, 2):
        s_copy(0, d).start()
    steps(1, early + late, 3, 4, False)
    for t in range(6):
        rs = pl.ds(t * 128, 128)
        vo[rs, :] = acc[1, rs, :].astype(BF)
    normalize(0, 0, 17, ko)
    w_a2()

    for i in range(5):
        @pl.when(c == 0)
        def _():
            for t in (0, 1):
                k_copy(t, i, partner).start()

        @pl.when(c == 1)
        def _():
            for t in (0, 1):
                k_copy(t, i, nxt).start()

    steps(2, early, 0, 4, True)
    w_b1()
    step_f2(2)
    steps(2, late, 0, 4, True)
    row_sq(2, 1)
    for d in (1, 3, 2):
        s_copy(1, d).start()
    normalize(1, 2, 16, qo)

    cols = pl.ds(pl.multiple_of(h * 1280, 1280), 1280)
    resid = (
        pltpu.make_async_copy(lat.at[:, cols], N.at[pl.ds(0, 768), pl.ds(0, 1280)], lsem.at[1]),
        pltpu.make_async_copy(ctl.at[:, cols], N.at[pl.ds(0, 768), pl.ds(1280, 1280)], lsem.at[2]),
    )
    for cp in resid:
        cp.start()

    mine = c == zl
    fold = HD ** -0.5 * 1.4426950408889634

    def attend_head(i):
        cs = head_cols(i)

        def tile(t, carry):
            s = t // 3
            rs = pl.ds(pl.multiple_of(t * 128, 128), 128)
            qt = qo[rs, cs]
            prior = pl.ds(pl.multiple_of(384 * (1 - s), 384), 384)
            here = pl.ds(pl.multiple_of(384 * s, 384), 384)
            far_k, far_v = pko[here, cs], pvo[here, cs]
            own_k, own_v = ko[here, cs], vo[here, cs]
            near_k = jnp.where(s == 0, pko[pl.ds(384, 384), cs], ko[pl.ds(0, 384), cs])
            near_v = jnp.where(s == 0, pvo[pl.ds(384, 384), cs], vo[pl.ds(0, 384), cs])
            blocks = []
            for kk in (far_k, near_k, own_k):
                blocks.append(lax.dot_general(qt, kk, (((1,), (1,)), ((), ())), preferred_element_type=F32))
            bs = [biaso[pl.ds(pl.multiple_of(8 * s, 8), 8), :][0:1, b * 384:b * 384 + 1] for b in range(3)]
            tops = [jnp.max(sc, axis=-1, keepdims=True) + bv for sc, bv in zip(blocks, bs)]
            top = jnp.maximum(jnp.maximum(tops[0], tops[1]), tops[2])
            total = None
            o = None
            for sc, bv, vv in zip(blocks, bs, (far_v, near_v, own_v)):
                ex = jnp.exp2((sc - (top - bv)) * fold)
                part = jnp.sum(ex, axis=-1, keepdims=True)
                pv = jnp.dot(ex.astype(BF), vv, preferred_element_type=F32)
                total = part if total is None else total + part
                o = pv if o is None else o + pv
            qo[rs, cs] = (o * (1.0 / total)).astype(BF)
            return carry

        lax.fori_loop(0, 6, tile, 0)

    def t_copy(d, i):
        src = qo.at[:, head_cols(i)]
        return remote(src, AT.at[z, :, head_cols(i)], tsem.at[d - 1, i], trsem.at[d - 1, i], place(x, y, z + d, c))

    def own_copy(i):
        return pltpu.make_async_copy(qo.at[:, head_cols(i)], AT.at[z, :, head_cols(i)], lsem.at[4 + i])

    def g_own(i):
        return remote(qo.at[:, head_cols(i)], AT.at[z, :, head_cols(i)], gsem.at[z, i], grsem.at[z, i], partner)

    def g_copy(g, i):
        ref = AT.at[g, :, head_cols(i)]
        return remote(ref, ref, gsem.at[g, i], grsem.at[g, i], partner)

    def send_head(i):
        @pl.when(mine)
        def _():
            t_copy(2, i).start()
            own_copy(i).start()
            g_own(i).start()

        @pl.when(jnp.logical_not(mine))
        def _():
            t_copy(1, i).start()
            t_copy(3, i).start()

    def pass_head(i):
        @pl.when(mine)
        def _():
            for d in (1, 3, 2):
                g = (z + 4 - d) % 4
                t_copy(d, i).wait_recv()
                g_copy(g, i).start()

    for i in range(5):
        for t in (0, 1):
            k_copy(t, i, partner).wait_recv()
        attend_head(i)
        send_head(i)
        if i == 1:
            w_b2()
        if i >= 2:
            pass_head(i - 2)
    pass_head(3)
    pass_head(4)

    @pl.when(mine)
    def _():
        for i in range(5):
            own_copy(i).wait()

    @pl.when(jnp.logical_not(mine))
    def _():
        for i in range(5):
            for g in range(4):
                g_copy(g, i).wait_recv()

    w_done()
    for cp in resid:
        cp.wait()

    def project_rows(r):
        rs = pl.ds(pl.multiple_of(r * 128, 128), 128)
        tot = None
        for g in range(4):
            t = lax.dot_general(
                AT[g, rs, :], WO[g].reshape(1280, 640), (((1,), (1,)), ((), ())), preferred_element_type=F32
            ).astype(BF).astype(F32)
            tot = t if tot is None else tot + t
        hid = N[rs, 0:1280].astype(F32) + N[rs, 1280:2560].astype(F32)
        return hid + gate[r // 3] * tot

    def h_copy(t):
        rs = pl.ds(pl.multiple_of(t * 128, 128), 128)
        return remote(shout.at[rs], shin.at[rs], hsem.at[t], hrsem.at[t], after)

    def odd_rows(t, carry):
        shout[pl.ds(pl.multiple_of(t * 128, 128), 128), :] = project_rows(t + 3).astype(BF)

        @pl.when(t > 0)
        def _():
            h_copy(t - 1).start()

        return carry

    lax.fori_loop(0, 3, odd_rows, 0)

    def even_rows(t, carry):
        out[1, pl.ds(pl.multiple_of(t * 128, 128), 128), :] = project_rows(t)

        @pl.when(t == 0)
        def _():
            h_copy(2).start()

        return carry

    lax.fori_loop(0, 3, even_rows, 0)
    for t in range(3):
        rs = pl.ds(t * 128, 128)
        h_copy(t).wait_recv()
        out[0, rs, :] = shin[rs, :].astype(F32)

    for t in range(3):
        h_copy(t).wait_send()
    for t in (0, 1):
        for i in range(5):
            k_copy(t, i, partner).wait_send()
    for k in (0, 1):
        for d in (1, 2, 3):
            s_copy(k, d).wait_send()
    for m in range(3):
        for half in (0, 1):
            for way in (0, 1):
                for part in (0, 1):
                    a_copy(m, half, way, part).wait_send()
                    b_copy(m, half, way, part).wait_send()
                a_relay(m, half, way).wait_send()
                b_relay(m, half, way).wait_send()
            for d in range(4):
                f_copy(m, half, d).wait_send()

    @pl.when(swapped)
    def _():
        for i in range(384 // LNB):
            x_copy(i, 1).wait_send()
            x_copy(i, 3).wait_send()

    for half, way in every:
        for part in (0, 1):
            wa_copy(half, way, part).wait_send()
            wb_copy(half, way, part).wait_send()
        wa_relay(half, way).wait_send()
        wb_relay(half, way).wait_send()

    @pl.when(y != h)
    def _():
        for t in (0, 1):
            remote(wo, spot, rsem.at[t], rrsem.at[zl], swapdev(t)).wait_send()

    @pl.when(y == h)
    def _():
        remote(wo, spot, rsem.at[0], rrsem.at[zl], swapdev(1 - zl)).wait_send()

    @pl.when(mine)
    def _():
        for i in range(5):
            t_copy(2, i).wait_send()
            g_own(i).wait_send()
            for d in (1, 2, 3):
                g_copy((z + 4 - d) % 4, i).wait_send()

    @pl.when(jnp.logical_not(mine))
    def _():
        for i in range(5):
            t_copy(1, i).wait_send()
            t_copy(3, i).wait_send()


def block(lat, ctl, mods, wk, wv, wq, bias, wo, gate):
    any_ = pl.BlockSpec(memory_space=pl.ANY)
    vm = pl.BlockSpec(memory_space=pltpu.VMEM)
    D = pltpu.SemaphoreType.DMA
    rows = pltpu.VMEM((768, 640), BF)
    stage2 = D((3, 2, 2, 3))
    return pl.pallas_call(
        block_kernel,
        out_shape=jax.ShapeDtypeStruct((2, 384, 1280), F32),
        in_specs=[any_, any_, vm, any_, any_, any_, any_, any_, vm],
        out_specs=vm,
        scratch_shapes=[
            pltpu.VMEM((3, 4, 4, 2, 160, 640), BF),
            pltpu.VMEM((1152, 5120), BF),
            pltpu.VMEM((2, LNB, 5120), BF),
            pltpu.VMEM((2, LNB, 5120), BF),
            pltpu.VMEM((3, 768, 640), F32),
            pltpu.VMEM((2, 8, 768), F32),
            pltpu.VMEM((2, 3, 8, 768), F32),
            rows, rows, rows, rows, rows,
            pltpu.VMEM((24, 1152), F32),
            pltpu.VMEM((4, 4, 2, 160, 640), BF),
            pltpu.VMEM((4, 768, 640), BF),
            pltpu.VMEM((384, 1280), BF),
            pltpu.VMEM((384, 1280), BF),
            D((2, 2)), D((3,)), D((3,)),
            stage2, stage2, stage2, stage2, D((3, 2, 4)), D((3, 2, 4)),
            D((2, 384 // LNB)), D((2, 384 // LNB)), D((2, 3)), D((2, 3)), D((2, 5)), D((2, 5)), D, D,
            D((2,)), D((2,)), D((2, 2, 3)), D((2, 2, 3)), D((2, 2, 3)), D((2, 2, 3)),
            D((3, 5)), D((3, 5)), D((4, 5)), D((4, 5)), D((9,)), D((3,)), D((3,)),
        ],
        compiler_params=pltpu.CompilerParams(
            collective_id=0, has_side_effects=True, vmem_limit_bytes=67043328
        ),
        name="block",
    )(lat, ctl, mods, wk, wv, wq, bias, wo, gate)


def shards(latents, control, levels, window_mask, modulation, w_query, w_key, w_value, w_out, q_gain, k_gain):
    owner = lax.axis_index("queue")
    head = lax.axis_index("head")
    lat = latents.reshape(768, 5120)
    ctl = control.reshape(768, 5120)
    mods = jnp.stack([lax.dynamic_index_in_dim(modulation, levels[s], 0, keepdims=False) for s in (0, 1)])
    gate = lax.dynamic_slice_in_dim(mods[:, 2:3], head * 1280, 1280, 2)
    ids = owner * 2 + jnp.arange(2, dtype=jnp.int32)
    seen = jnp.stack(
        [(window_mask[:, 0] == 1) & (ids >= 2), (window_mask[:, 1] == 1) & (ids >= 1), jnp.ones((2,), dtype=bool)],
        axis=1,
    )
    bias = jnp.where(jnp.repeat(seen, 384, axis=1), 0.0, -1e30).astype(F32)
    bias = jnp.broadcast_to(bias[:, None, :], (2, 8, 1152)).reshape(16, 1152)
    gains = jnp.pad(jnp.stack([q_gain, k_gain]), ((0, 6), (0, 512)))
    bias = jnp.concatenate([bias, gains], axis=0)
    return block(lat, ctl, mods[:, 0:2], w_key, w_value, w_query, bias, w_out.T, gate)


def solution(mesh):
    placed = (
        P("queue", None, None),
        P("queue", None, None),
        P("queue"),
        P("queue", None),
        P(),
        P("queue", "head"),
        P("queue", "head"),
        P("queue", "head"),
        P("head", "queue"),
        P("head"),
        P("head"),
    )
    return jax.shard_map(
        shards, mesh=mesh, in_specs=placed, out_specs=P("queue", None, "head"), check_vma=False
    )
```

time: 248 us -> 192 us (0.77)
  Pallas kernels: 203 us -> 176 us
  waiting for transfers between devices: 21.7 us -> 0 us
  starting transfers between devices: 2.9 us -> 0 us
    pallas_call x3 -> x1, Pallas kernels: 203 us -> 176 us  [block(): pl.pallas_call(block_kernel, out_shape=jax.ShapeDtypeStruct((2, 384, 1280...]
    ppermute x1 -> x0, waiting for transfers between devices: 21.7 us -> none  [shards(): last = lax.ppermute(updated[384:].astype(BF), 'queue', pairs).astype(F32)]
    ppermute x1 -> x0, starting transfers between devices: 2.9 us -> none  [shards(): last = lax.ppermute(updated[384:].astype(BF), 'queue', pairs).astype(F32)]
  transfers between devices with their start and end apart: 1 -> 0, of which waited for: 1 -> 0; matrix products, arithmetic and copies ran while one was open for 0% -> 0% of each run, Pallas kernels for 0% -> 0%
where the time goes in v3:
time: 192 us; the launch traced here: 191 us
  Pallas kernels  176 us (92%)
  local copies, waits for them, and re-layouts  9.76 us (5%)
  between operations  3.89 us (2%)
    pallas_call x1, Pallas kernels, block(): pl.pallas_call(block_kernel, out_shape=jax.ShapeDtypeStruct((2, 384, 1280...  176 us
    unnamed x4, local copies, waits for them, and re-layouts  4.39 us

profile of v3, /device:TPU:0, one launch (start us, length us, event | category | flops | bytes accessed | tf_op | source)
XLA Modules:
  0.0 191.0 jit_solution(17155429809956364165)
XLA Ops:
  0.0 0.1 pad.11.clone
  0.1 0.8 compare_and_fusion.1
  0.9 0.1 add_select_fusion
  1.0 1.3 fusion
  6.1 0.7 stack.21
  6.8 0.7 stack.22
  7.5 0.1 broadcast_bitcast_fusion.1
  7.6 0.7 pad_maximum_fusion.bias
  8.3 1.3 constant_dynamic-slice_fusion.1
  9.7 0.7 slice.24.mods
  10.3 0.6 constant_dynamic-slice_fusion.gate
  10.9 175.8 %block.1 = f32[2,384,1280]{2,1,0:T(8,128)} custom-call(bf16[768,5120]{1,0:T(8,128)(2,1)} %bitcast.11, bf16[768,5120]{1,0:T(8,128)(2,1)} %bitcast.12, f32[2,2,5120]{2,1,0:T(2,128)} %slice.24.mods, bf16[160,640]{1,0:T(8,128)(2,1)} %wk.1, bf16[160,640]{1,0:T(8,128)(2,1)} %wv.1, bf16[160,640]{1,0:T(8,128)(2,1)} %wq.1, f32[24,1152]{1,0:T(8,128)} %pad_maximum_fusion.bias, ...), custom_call_target="tpu_custom_call" | custom-call | tf_op jit(solution)/shard_map/block/pallas_call | solution.py:719
  186.7 4.3 %copy.23 = f32[2,384,1280]{2,1,0:T(8,128)} copy(f32[2,384,1280]{2,1,0:T(8,128)} %block.1) | data formatting | bytes 7864320
  (6 shorter events, 0.1 us)
